TPU v7x, 512 devices: a whole 4x8x8 slice. The times are simulated.
512 devices in a mesh: row: 32 (over x, z_lo, core), col: 16 (over z_hi, y).
Axes of the slice: x: 4, y: 8, z: 8 (z_hi: 2, z_lo: 4; z = z_hi * 4 + z_lo), core: 2. Of those that a mesh axis runs over, the one named last changes fastest.
Arguments:
- cached_inverse: float32 [4, 32, 128, 8, 16, 128], P(None, 'row', None, None, 'col'), may hold values from -6 to 6
- parent_panel: float32 [256, 96, 128], P('col', 'row'), may hold values from -0.046875 to 0.046875
- parent_blocks: int32 [96], P('row'), may hold values from -1 to 127, as said below
- parent_sizes: int32 [96], P('row'), may hold values from 0 to 128, as said below
- parent_diagonal: float32 [256, 256], P('col'), may hold values from -6 to 6
- child_panel: float32 [256, 96, 128], P('col', 'row'), may hold values from -0.046875 to 0.046875
- child_top: float32 [256, 256], P('col'), may hold values from -0.375 to 0.375
- child_blocks: int32 [96], P('row'), may hold values from -1 to 127, as said below
- child_sizes: int32 [96], P('row'), may hold values from 0 to 128, as said below
- child_diagonal: float32 [256, 256], P('col'), may hold values from -6 to 6
Outputs:
- parent_rows: float32 [4, 32, 128, 256], P(None, 'row', 'col')
- parent_diag: float32 [256, 256], P('col')
- child_rows: float32 [4, 32, 128, 256], P(None, 'row', 'col')
- child_upper: float32 [256, 256], P('col')
- child_diag: float32 [256, 256], P('col')
Inputs may be any that keep to these rules, and one draw needn't show every extreme that they name: `parent_blocks`: slots p*3 to p*3 + 2 belong to index p of row; their live slots come first, name distinct block numbers congruent to p modulo the size of row, and the rest hold -1. Some index of row has 3 live slots. `parent_sizes`: 0 exactly for the slots that hold -1 in parent_blocks. `child_blocks`: slot k holds either parent_blocks[k] (a live parent slot) or -1. `child_sizes`: 0 exactly for the slots that hold -1 in child_blocks, else at most parent_sizes of the same slot.
All inputs are finite; a program needn't handle non-finite values.
Results may differ from a plain program's by a relative error of at most 0.000096.
Values sent between devices are 32-bit elements; how exact they have to be, the bound alone decides.
A program may use at most 64 MiB of HBM per device.

v0:
```python
import jax
import jax.numpy as jnp
from jax import lax
from jax.sharding import PartitionSpec as P

highest = lax.Precision.HIGHEST


def from_root(value, axis, source):
    kept = jnp.where(lax.axis_index(axis) == source, value, 0).astype(value.dtype)
    return lax.psum(kept, axis)


def live_rows(sizes, block_rows):
    return (jnp.arange(block_rows, dtype=jnp.int32)[None, :] < sizes[:, None]).astype(jnp.float32)


def own_share(widened, blocks, row_live, row_index, row_total, col_index, row_share, local_rows):
    wanted = jnp.arange(local_rows, dtype=jnp.int32) * row_total + row_index
    onehot = (blocks[None, :] == wanted[:, None]).astype(jnp.float32)
    sliced = lax.dynamic_slice_in_dim(widened, col_index * row_share, row_share, 2)
    own_rows = jnp.einsum("rk,wkb->rbw", onehot, sliced, precision=highest)
    live_part = lax.dynamic_slice_in_dim(row_live, col_index * row_share, row_share, 1)
    row_alive = jnp.einsum("rk,kb->rb", onehot, live_part, precision=highest)
    return (own_rows, row_alive)


def add_columns(column_dense, widened, blocks, col_index, col_total):
    wanted = jnp.arange(column_dense.shape[0], dtype=jnp.int32) * col_total + col_index
    onehot = (blocks[None, :] == wanted[:, None]).astype(jnp.float32)
    return column_dense + jnp.einsum("ck,wky->cwy", onehot, widened, precision=highest)


def column_panel(widened, blocks, col_index, col_total, row_total, col_blocks):
    column_dense = jnp.zeros((col_blocks, widened.shape[0], widened.shape[2]), jnp.float32)
    for repeat in range(row_total // col_total):
        sender = col_index + repeat * col_total
        heard_panel, heard_blocks = (
            from_root(widened, "row", sender),
            from_root(blocks, "row", sender),
        )
        column_dense = add_columns(column_dense, heard_panel, heard_blocks, col_index, col_total)
    return column_dense


def child_panels(
    child_panel, child_top, child_live, child_blocks, col_index, col_total, row_total, col_blocks
):
    wide_child, top_full = (
        lax.all_gather(child_panel, "col", axis=0, tiled=True),
        lax.all_gather(child_top, "col", axis=0, tiled=True),
    )
    child_full = wide_child * child_live[None, :, :]
    child_dense = column_panel(
        child_full, child_blocks, col_index, col_total, row_total, col_blocks
    )
    return (child_full, child_dense, top_full)


def apply_inverse(cached, column_dense):
    summed = lax.psum_scatter(
        jnp.einsum(
            "rxcy,cwy->xrw",
            cached,
            column_dense,
            precision=highest,
            preferred_element_type=jnp.float32,
        ),
        "col",
        scatter_dimension=0,
        tiled=True,
    )
    return jnp.transpose(summed, (1, 0, 2))


def diagonal_sum(partial_rows, panel_width, col_share, col_index):
    entire = lax.psum(partial_rows(0, panel_width), ("row", "col"))
    return lax.dynamic_slice_in_dim(entire, col_index * col_share, col_share, 0)


def body(
    cached_inverse,
    parent_panel,
    parent_blocks,
    parent_sizes,
    parent_diagonal,
    child_panel,
    child_top,
    child_blocks,
    child_sizes,
    child_diagonal,
):
    row_total = lax.axis_size("row")
    col_total = lax.axis_size("col")
    row_index = lax.axis_index("row")
    col_index = lax.axis_index("col")
    local_rows = cached_inverse.shape[0]
    block_rows = cached_inverse.shape[2]
    col_blocks = cached_inverse.shape[3]
    cached = cached_inverse.reshape(local_rows, block_rows, col_blocks, block_rows)
    panel_width = parent_diagonal.shape[1]
    row_share = block_rows // col_total
    col_share = panel_width // col_total
    parent_live = live_rows(parent_sizes, block_rows)
    child_live = live_rows(child_sizes, block_rows)
    wide_parent = lax.all_gather(parent_panel, "col", axis=0, tiled=True)
    parent_full = wide_parent * parent_live[None, :, :]
    parent_dense = column_panel(
        parent_full, parent_blocks, col_index, col_total, row_total, col_blocks
    )
    parent_own, parent_alive = own_share(
        parent_full,
        parent_blocks,
        parent_live,
        row_index,
        row_total,
        col_index,
        row_share,
        local_rows,
    )
    parent_local = -apply_inverse(cached, parent_dense) * parent_alive[:, :, None]

    def parent_terms(offset, amount):
        return jnp.einsum("rbw,rbv->wv", parent_own, parent_local, precision=highest)

    parent_diag = parent_diagonal - diagonal_sum(parent_terms, panel_width, col_share, col_index)
    child_full, child_dense, top_full = child_panels(
        child_panel,
        child_top,
        child_live,
        child_blocks,
        col_index,
        col_total,
        row_total,
        col_blocks,
    )
    child_own, child_alive = own_share(
        child_full, child_blocks, child_live, row_index, row_total, col_index, row_share, local_rows
    )
    carried = jnp.einsum("rbw,wv->rbv", parent_local, top_full, precision=highest)
    child_local = -(apply_inverse(cached, child_dense) + carried) * child_alive[:, :, None]

    def upper_terms(offset, amount):
        return jnp.einsum("rbw,rbv->wv", parent_local, child_own, precision=highest)

    upper_sum = diagonal_sum(upper_terms, panel_width, col_share, col_index)
    child_upper = -(
        jnp.dot(parent_diag, top_full, precision=highest, preferred_element_type=jnp.float32)
        + upper_sum
    )
    leading = (row_index == 0).astype(jnp.float32)

    def child_terms(offset, amount):
        first_term = jnp.einsum("kc,kv->cv", child_top, child_upper, precision=highest) * leading
        return first_term + jnp.einsum("rbc,rbv->cv", child_own, child_local, precision=highest)

    child_diag = child_diagonal - diagonal_sum(child_terms, panel_width, col_share, col_index)
    return (
        parent_local[:, None, :, :],
        parent_diag,
        child_local[:, None, :, :],
        child_upper,
        child_diag,
    )


def solution(mesh):
    in_specs = (
        P(None, "row", None, None, "col", None),
        P("col", "row", None),
        P("row"),
        P("row"),
        P("col", None),
        P("col", "row", None),
        P("col", None),
        P("row"),
        P("row"),
        P("col", None),
    )
    out_specs = (
        P(None, "row", "col", None),
        P("col", None),
        P(None, "row", "col", None),
        P("col", None),
        P("col", None),
    )
    return jax.shard_map(body, mesh=mesh, in_specs=in_specs, out_specs=out_specs, check_vma=False)
```

profile of v0, /device:TPU:1, one launch (start us, length us, event | category | flops | bytes accessed | tf_op | source)
XLA Modules:
  0.0 1194.0 jit_solution(474740232066148281)
XLA Ops:
  7.2 0.0 copy-start
  7.2 0.0 all-reduce.15.cloned.1.call-start
  7.2 1.4 iota_compare_fusion.1
  8.7 1.3 iota_compare_fusion
  9.9 54.9 %all_gather.9 = f32[256,3,128]{2,0,1:T(8,128)S(1)} all-gather(f32[16,3,128]{2,0,1:T(8,128)} %param.11), channel_id=1, replica_groups=mesh['row'=32,'col'=16] {'col'}, dimensions={0}, use_global_device_ids=true | all-gather | bytes 417792 | tf_op jit(solution)/shard_map/all_gather | solution.py:106
  64.9 1.0 copy.31
  65.9 43.0 %all_gather.10 = f32[256,3,128]{2,0,1:T(8,128)S(1)} all-gather(f32[16,3,128]{2,0,1:T(8,128)} %param.15), channel_id=1, replica_groups=mesh['row'=32,'col'=16] {'col'}, dimensions={0}, use_global_device_ids=true | all-gather | bytes 417792 | tf_op jit(solution)/shard_map/all_gather | solution.py:50
  108.9 0.2 copy.36
  109.1 1.0 broadcast_select_fusion.1
  110.2 2.1 broadcast_select_fusion.3
  112.2 1.2 broadcast_select_fusion
  113.5 0.0 all-reduce.15.cloned.1.call-update
  113.5 0.0 all-reduce.17.cloned.1.call-start
  113.5 0.0 copy-done.8
  113.6 0.0 copy-done.9
  113.6 25.1 %all-reduce.2 = (s32[3]{0:T(128)S(1)}, s32[3]{0:T(128)S(1)}, s32[3]{0:T(128)S(1)}, s32[3]{0:T(128)S(1)}) all-reduce(s32[3]{0:T(128)S(1)} %get-tuple-element.39, s32[3]{0:T(128)S(1)} %get-tuple-element.40, s32[3]{0:T(128)S(1)} %get-tuple-element.36, s32[3]{0:T(128)S(1)} %get-tuple-element.35), channel_id=1, replica_groups=mesh['row'=32,'col'=16] {'row'}, use_global_device_ids=true, to_apply=%region_2.3 | all-reduce | flops 12 | bytes 96 | tf_op jit(solution)/shard_map/psum | solution.py:11
  138.7 273.4 %all-reduce.15.cloned.1.call-done = (f32[256,3,128]{0,1,2:T(4,128)}, f32[256,3,128]{0,1,2:T(4,128)}, f32[256,3,128]{0,1,2:T(4,128)}, f32[256,3,128]{0,1,2:T(4,128)}) async-done(((f32[256,3,128]{0,1,2:T(4,128)}, f32[256,3,128]{0,1,2:T(4,128)}, f32[256,3,128]{0,1,2:T(4,128)}, f32[256,3,128]{0,1,2:T(4,128)}), (f32[256,3,128]{0,1,2:T(4,128)}, f32[256,3,128]{0,1,2:T(4,128)}, f32[256,3,128]{0,1,2:T(4,128)}, ...) | async-done | bytes 1572880 | tf_op jit(solution)/shard_map/psum | solution.py:11
  412.1 2.0 copy.51
  414.1 2.1 copy.49
  416.2 1.7 fusion.34
  417.9 1.7 fusion.36
  419.5 0.0 copy-done
  419.5 3.2 fusion.4
  422.8 2.1 copy.33
  424.8 2.1 copy.58
  426.9 2.0 copy.56
  429.0 1.7 fusion.30
  430.6 1.7 fusion.32
  432.3 3.2 fusion.7
  435.5 2.1 copy.38
  437.6 0.0 all-reduce.17.cloned.1.call-update
  437.6 0.0 all-reduce.13.cloned.1.call-start
  437.7 0.5 multiply_add_fusion
  438.2 0.0 copy-done.6
  438.2 0.1 copy.45
  438.3 1.3 dynamic-slice
  440.2 0.0 copy-done.3
  440.2 46.7 %all_gather.11 = f32[256,256]{1,0:T(8,128)S(1)} all-gather(f32[16,256]{1,0:T(8,128)S(1)} %copy-done.3), channel_id=1, replica_groups=mesh['row'=32,'col'=16] {'col'}, dimensions={0}, use_global_device_ids=true | all-gather | bytes 278528 | tf_op jit(solution)/shard_map/all_gather | solution.py:51
  486.9 1.5 fusion.38
  488.4 1.5 fusion.42
  489.8 1.5 convolution_bitcast_fusion.3
  491.3 0.9 fusion.26
  492.2 133.2 %all-reduce.17.cloned.1.call-done = (f32[128,4,256]{2,1,0:T(4,128)}, f32[128,4,256]{2,1,0:T(4,128)}) async-done(((f32[128,4,256]{2,1,0:T(4,128)}, f32[128,4,256]{2,1,0:T(4,128)}), (f32[128,4,256]{2,1,0:T(4,128)}, f32[128,4,256]{2,1,0:T(4,128)})) %all-reduce.17.cloned.1.call-update) | async-done | bytes 1048592
  625.4 0.8 constant_dynamic-slice_fusion
  626.2 0.8 fusion.21
  627.0 1.1 convolution_bitcast_fusion.2
  628.1 1.9 convolution_bitcast_fusion.1
  630.0 0.0 all-reduce.13.cloned.1.call-update
  630.1 0.0 all-reduce.11.cloned.1.call-start
  630.1 0.9 fusion.13
  631.0 0.0 copy-start.2
  631.1 0.4 convolution_bitcast_fusion
  631.5 281.6 %all-reduce.13.cloned.1.call-done = (f32[256,256]{1,0:T(8,128)}, f32[256,256]{1,0:T(8,128)}) async-done(((f32[256,256]{1,0:T(8,128)}, f32[256,256]{1,0:T(8,128)}), (f32[256,256]{1,0:T(8,128)}, f32[256,256]{1,0:T(8,128)})) %all-reduce.13.cloned.1.call-update) | async-done | bytes 524304 | tf_op jit(solution)/shard_map/psum | solution.py:77
  913.1 0.7 dynamic-slice_subtract_fusion.1
  913.8 1.0 fusion.14
  914.8 0.0 copy-start.5
  914.8 1.1 fusion.11
  915.9 0.0 all-reduce.11.cloned.1.call-update
  915.9 0.8 fusion.81
  916.8 0.6 copy.46
  917.4 268.4 %all-reduce.11.cloned.1.call-done = f32[256,256]{0,1:T(8,128)} async-done(((f32[256,256]{0,1:T(8,128)}), f32[256,256]{0,1:T(8,128)}) %all-reduce.11.cloned.1.call-update) | async-done | bytes 262160 | tf_op jit(solution)/shard_map/psum | solution.py:77
  1185.8 1.0 dynamic-slice_subtract_fusion
  1186.8 0.7 copy.48
  1187.5 0.0 copy-done.5
  (13 shorter events, 0.0 us)
Async XLA Ops:
  7.2 412.4 %copy-start = (f32[4,1,128,8,1,128]{5,4,3,2,1,0:T(1,128)S(1)}, f32[4,1,128,8,1,128]{5,4,3,2,1,0:T(1,128)}, u32[]{:S(2)}) copy-start(f32[4,1,128,8,1,128]{5,4,3,2,1,0:T(1,128)} %param.10) | copy-start | bytes 6291460
  7.2 404.9 %all-reduce.15.cloned.1.call-start = ((), (), s32[]{:S(2)}) async-start(), calls=%async_computation.2 | async-start | bytes 4194304 | tf_op jit(solution)/shard_map/psum | solution.py:11
  112.2 1.3 copy-start.8
  112.2 1.3 copy-start.9
  113.5 511.9 %all-reduce.17.cloned.1.call-start = ((), (), s32[]{:S(2)}) async-start(), calls=%async_computation.3 | async-start | bytes 2097152
  435.5 2.6 copy-start.6
  435.5 4.7 copy-start.3
  437.6 475.4 %all-reduce.13.cloned.1.call-start = ((), (), s32[]{:S(2)}) async-start(), calls=%async_computation.1 | async-start | bytes 1048576 | tf_op jit(solution)/shard_map/psum | solution.py:77
  491.3 139.7 %copy-start.1 = (f32[4,8,256]{2,0,1:T(4,128)S(1)}, f32[4,8,256]{2,0,1:T(4,128)}, u32[]{:S(2)}) copy-start(f32[4,8,256]{2,0,1:T(4,128)} %convolution_bitcast_fusion.3) | copy-start | bytes 98308
  491.3 424.6 %copy-start.7 = (f32[4,8]{0,1:T(8,128)S(1)}, f32[4,8]{0,1:T(8,128)}, u32[]{:S(2)}) copy-start(f32[4,8]{0,1:T(8,128)} %fusion.42) | copy-start | bytes 388
  630.1 555.7 %all-reduce.11.cloned.1.call-start = ((), (), s32[]{:S(2)}) async-start(), calls=%async_computation | async-start | bytes 524288 | tf_op jit(solution)/shard_map/psum | solution.py:77
  631.0 556.4 %copy-start.2 = (f32[4,8,256]{2,1,0:T(8,128)}, f32[4,8,256]{2,1,0:T(8,128)S(1)}, u32[]{:S(2)}) copy-start(f32[4,8,256]{2,1,0:T(8,128)S(1)} %fusion.13) | copy-start | bytes 98308
  913.8 273.7 %copy-start.4 = (f32[16,256]{1,0:T(8,128)}, f32[16,256]{1,0:T(8,128)S(1)}, u32[]{:S(2)}) copy-start(f32[16,256]{1,0:T(8,128)S(1)} %dynamic-slice_subtract_fusion.1) | copy-start | bytes 49156
  914.8 272.7 %copy-start.5 = (f32[16,256]{1,0:T(8,128)}, f32[16,256]{1,0:T(8,128)S(1)}, u32[]{:S(2)}) copy-start(f32[16,256]{1,0:T(8,128)S(1)} %fusion.14) | copy-start | bytes 49156
Sparse Core Ops, SparseCore 0:
  113.6 298.4 all-reduce.14
  437.7 187.6 all-reduce.16
  630.6 282.4 all-reduce.12
  917.9 267.8 all-reduce.10
where the time goes:
time: 1200 us; the launch traced here: 1190 us
  waiting for transfers between devices  957 us (80%)
  blocking collectives  170 us (14%)
  matrix products  24.9 us (2%)
  local copies, waits for them, and re-layouts  17 us (1%)
  between operations  14.6 us (1%)
    psum x2, waiting for transfers between devices, diagonal_sum(): entire = lax.psum(partial_rows(0, panel_width), ('row', 'col'))  550 us
    psum x1, waiting for transfers between devices, from_root(): return lax.psum(kept, axis)  273 us
    unnamed x5, waiting for transfers between devices  133 us
    all_gather x1, blocking collectives, body(): wide_parent = lax.all_gather(parent_panel, 'col', axis=0, tiled=True)  54.9 us
    all_gather x1, blocking collectives, child_panels(): lax.all_gather(child_top, 'col', axis=0, tiled=True)  46.7 us
    all_gather x1, blocking collectives, child_panels(): lax.all_gather(child_panel, 'col', axis=0, tiled=True)  43 us
    psum x1, blocking collectives, from_root(): return lax.psum(kept, axis)  25.1 us
  transfers between devices with their start and end apart: 4, of which 4 were waited for; matrix products, arithmetic and copies ran while one was open for 1% of the time, Pallas kernels for 0%

commit v1 on v0

v1 whole, which is shorter than its diff:
```python
import jax
import jax.numpy as jnp
from jax import lax
from jax.experimental import pallas as pl
from jax.experimental.pallas import tpu as pltpu
from jax.sharding import PartitionSpec as P

MESH = pl.DeviceIdType.MESH
F32 = jnp.float32
BF16 = jnp.bfloat16

NX, NZL, NZH, NY, NK = 4, 4, 2, 8, 2
NZ = NZL * NZH
NROW, NCOL = NX * NZL * NK, NZH * NY
W, B, SL, RC = 256, 128, 3, 4
SHARE = W // NCOL
ROWS = SL * B
CB = B // NCOL
PATCH = 2 * ROWS + 128
OWN = W + 2 * ROWS


def place():
    p = lax.axis_index("row")
    q = lax.axis_index("col")
    x = p // (NZL * NK)
    zl = (p // NK) % NZL
    k = p % NK
    return p, q, x, zl, k, q // NY, q % NY


def row_id(x, zl, k):
    return (x * NZL + zl) * NK + k


def rcopy(src, dst, send, recv, target):
    return pltpu.make_async_remote_copy(
        src_ref=src,
        dst_ref=dst,
        send_sem=send,
        recv_sem=recv,
        device_id=target,
        device_id_type=MESH,
    )


def spread_kernel(
    x_ref, g_ref, c_ref, ps, pr, lsem, zs, zr, xs, xr, ks, kr, hs, hr, us, ur, ds, dr
):
    p, q, x, zl, k, zh, y = place()
    half, cls = p // NCOL, p % NCOL
    fixed = q == cls
    swap = (half * NCOL + q, cls)
    core = (row_id(x, zl, 1 - k), q)
    zdev = [None] + [(row_id(x, (zl + d) % NZL, k), q) for d in range(1, NZL)]
    xdev = [None] + [(row_id((x + d) % NX, zl, k), q) for d in range(1, NX)]
    hdev = (p, (1 - zh) * NY + y)
    up = (p, zh * NY + (y + 1) % NY)
    down = (p, zh * NY + (y + NY - 1) % NY)

    barrier = pltpu.get_barrier_semaphore()
    for dev in zdev[1:] + xdev[1:] + [core, hdev, up, down]:
        pl.semaphore_signal(barrier, inc=1, device_id=dev, device_id_type=MESH)

    @pl.when(jnp.logical_not(fixed))
    def _():
        pl.semaphore_signal(barrier, inc=1, device_id=swap, device_id_type=MESH)

    pl.semaphore_wait(barrier, NZL - 1 + NX - 1 + 4 + jnp.where(fixed, 0, 1))

    sends = []

    def send(*args):
        copy = rcopy(*args)
        copy.start()
        sends.append(copy)

    piece = x_ref.at[:, W : W + PATCH]
    mine = x_ref.at[:, 0:OWN]

    out = rcopy(piece, g_ref.at[half * NCOL + q], ps.at[0], pr.at[0], swap)
    local = pltpu.make_async_copy(piece, g_ref.at[p], lsem.at[0])

    @pl.when(jnp.logical_not(fixed))
    def _():
        out.start()

    @pl.when(fixed)
    def _():
        local.start()

    def ring(a, t, src_up, src_down):
        zz = zh if a == 0 else 1 - zh
        if src_up is not None:
            at = zz * NY + (y + NY - t) % NY
            send(src_up, c_ref.at[at], us.at[a * 4 + t], ur.at[a * 4 + t], up)
        if src_down is not None:
            at = zz * NY + (y + t) % NY
            send(src_down, c_ref.at[at], ds.at[a * 3 + t], dr.at[a * 3 + t], down)

    def ring_up_wait(a, t):
        zz = zh if a == 0 else 1 - zh
        got = c_ref.at[zz * NY + (y + NY - 1 - t) % NY]
        rcopy(got, got, us.at[a * 4 + t], ur.at[a * 4 + t], up).wait_recv()
        if t < 3:
            ring(a, t + 1, got, None)

    def ring_down_wait(a, t):
        zz = zh if a == 0 else 1 - zh
        got = c_ref.at[zz * NY + (y + 1 + t) % NY]
        rcopy(got, got, ds.at[a * 3 + t], dr.at[a * 3 + t], down).wait_recv()
        if t < 2:
            ring(a, t + 1, None, got)

    send(mine, c_ref.at[q], hs.at[0], hr.at[0], hdev)
    ring(0, 0, mine, mine)
    c_ref[q] = x_ref[:, 0:OWN]

    ring_up_wait(0, 0)
    ring_down_wait(0, 0)
    other = c_ref.at[(1 - zh) * NY + y]
    rcopy(other, other, hs.at[0], hr.at[0], hdev).wait_recv()
    ring(1, 0, other, other)

    @pl.when(jnp.logical_not(fixed))
    def _():
        rcopy(piece, g_ref.at[p], ps.at[0], pr.at[0], swap).wait_recv()

    @pl.when(fixed)
    def _():
        local.wait()

    def fan(src, dz):
        got = g_ref.at[src]
        for d in range(1, NX):
            send(got, got, xs.at[dz * 3 + d - 1], xr.at[dz * 3 + d - 1], xdev[d])
        send(got, got, ks.at[dz * 4], kr.at[dz * 4], core)

    own = g_ref.at[p]
    for d in range(1, NZL):
        send(own, own, zs.at[d - 1], zr.at[d - 1], zdev[d])
    fan(p, 0)

    def z_wait(d):
        src = row_id(x, (zl + NZL - d) % NZL, k)
        got = g_ref.at[src]
        rcopy(got, got, zs.at[d - 1], zr.at[d - 1], zdev[d]).wait_recv()
        fan(src, d)

    def x_wait(dz, d):
        src = row_id((x + NX - d) % NX, (zl + NZL - dz) % NZL, k)
        got = g_ref.at[src]
        rcopy(got, got, xs.at[dz * 3 + d - 1], xr.at[dz * 3 + d - 1], xdev[d]).wait_recv()
        send(got, got, ks.at[dz * 4 + d], kr.at[dz * 4 + d], core)

    ring_up_wait(0, 1)
    ring_down_wait(0, 1)
    ring_up_wait(1, 0)
    ring_down_wait(1, 0)
    z_wait(1)
    z_wait(3)
    ring_up_wait(0, 2)
    ring_up_wait(1, 1)
    ring_down_wait(1, 1)
    z_wait(2)
    for d in (1, 3, 2):
        x_wait(0, d)
    ring_up_wait(1, 2)
    for dz in (1, 3, 2):
        for d in (1, 3, 2):
            x_wait(dz, d)
    ring_down_wait(0, 2)
    ring_up_wait(0, 3)
    ring_down_wait(1, 2)
    ring_up_wait(1, 3)
    for dz in range(NZL):
        for d in range(NX):
            src = row_id((x + NX - d) % NX, (zl + NZL - dz) % NZL, 1 - k)
            got = g_ref.at[src]
            rcopy(got, got, ks.at[dz * 4 + d], kr.at[dz * 4 + d], core).wait_recv()

    @pl.when(jnp.logical_not(fixed))
    def _():
        out.wait_send()

    for copy in sends:
        copy.wait_send()


def spread(pieces):
    vmem = pl.BlockSpec(memory_space=pltpu.VMEM)
    dma = pltpu.SemaphoreType.DMA
    return pl.pallas_call(
        spread_kernel,
        out_shape=(
            jax.ShapeDtypeStruct((NROW, SHARE, PATCH), F32),
            jax.ShapeDtypeStruct((NCOL, SHARE, OWN), F32),
        ),
        in_specs=[vmem],
        out_specs=(vmem, vmem),
        scratch_shapes=[
            dma((1,)), dma((1,)), dma((1,)),
            dma((3,)), dma((3,)),
            dma((12,)), dma((12,)),
            dma((16,)), dma((16,)),
            dma((1,)), dma((1,)),
            dma((8,)), dma((8,)),
            dma((6,)), dma((6,)),
        ],
        compiler_params=pltpu.CompilerParams(collective_id=0, has_side_effects=True),
        name="spread",
    )(pieces)


def halves(a):
    hi = a.astype(BF16)
    lo = (a - hi.astype(F32)).astype(BF16)
    return hi, lo


def dot3(a, b, dims):
    def one(u, v):
        return lax.dot_general(u, v, (dims, ((), ())), preferred_element_type=F32)

    return one(a[0], b[0]) + (one(a[0], b[1]) + one(a[1], b[0]))


NN = ((1,), (0,))
NT = ((1,), (1,))


def multiply_kernel(idx, s_ref, g_ref, c_ref, d_ref, yz_ref, aue_ref, sub, yv, zv, uv):
    for s in range(SL):
        for t in range(2 * SL):
            start = idx[s] * (B * 8) + idx[SL + t]
            sub[s * B : (s + 1) * B, t * B : (t + 1) * B] = s_ref[pl.ds(start, B, stride=8), :]
    gp = [halves(g_ref[h, :, 0:ROWS]) for h in range(2)]
    gq = [halves(g_ref[h, :, ROWS : 2 * ROWS]) for h in range(2)]
    top = halves(c_ref[:, 0:W])
    rows = lax.broadcasted_iota(jnp.int32, (B, 1), 0)
    for s in range(SL):
        at = slice(s * B, (s + 1) * B)
        left = [halves(sub[at, h * ROWS : (h + 1) * ROWS]) for h in range(2)]
        yp = dot3(left[0], gp[0], NT) + dot3(left[1], gp[1], NT)
        y = jnp.where(rows < idx[9 + s], -yp, 0.0)
        zq = dot3(left[0], gq[0], NT) + dot3(left[1], gq[1], NT)
        z = jnp.where(rows < idx[12 + s], -(zq + dot3(halves(y), top, NN)), 0.0)
        yv[at, :] = y
        zv[at, :] = z
        yz_ref[:, s * CB : (s + 1) * CB, 0:W] = y.reshape(NCOL, CB, W)
        yz_ref[:, s * CB : (s + 1) * CB, W : 2 * W] = z.reshape(NCOL, CB, W)
    pp = halves(c_ref[:, W : W + ROWS])
    qp = halves(c_ref[:, W + ROWS : OWN])
    y = halves(yv[...])
    a = dot3(pp, y, NN)
    uv[...] = dot3(halves(a), top, NN) - dot3(qp, y, NN).T

    @pl.when(idx[16] == 1)
    def _():
        own = pl.ds(pl.multiple_of(idx[15], SHARE), SHARE)
        uv[own, :] = uv[own, :] - dot3(halves(d_ref[...]), top, NN)

    u = uv[...]
    e = -dot3(halves(c_ref[:, 0:W].T), halves(u), NN) - dot3(qp, halves(zv[...]), NN)
    for m, mat in enumerate((a, u, e)):
        for k in range(2):
            aue_ref[k, m] = mat[:, k * 128 : (k + 1) * 128]


def multiply(idx, s, g, c, d):
    vmem = pl.BlockSpec(memory_space=pltpu.VMEM)
    return pl.pallas_call(
        multiply_kernel,
        out_shape=(
            jax.ShapeDtypeStruct((NCOL, SL * CB, 2 * W), F32),
            jax.ShapeDtypeStruct((2, 3, W, 128), F32),
        ),
        in_specs=[pl.BlockSpec(memory_space=pltpu.SMEM), vmem, vmem, vmem, vmem],
        out_specs=(vmem, vmem),
        scratch_shapes=[
            pltpu.VMEM((ROWS, 2 * ROWS), F32),
            pltpu.VMEM((ROWS, W), F32),
            pltpu.VMEM((ROWS, W), F32),
            pltpu.VMEM((W, W), F32),
        ],
        name="multiply",
    )(idx, s, g, c, d)


def gather_kernel(
    yz_ref, aue_ref, yzo, auo,
    kbuf, acc, xbuf, accx, ybuf, accy, zbuf, yzbuf, yzacc, hbuf,
    ks, kr, xs, xr, ys, yr, zs, zr, fs, fr, vs, vr, hs, hr,
):
    p, q, x, zl, k, zh, y = place()
    z = zh * NZL + zl
    xk = {}
    for d in range(NX):
        for f in range(2):
            if d or f:
                xk[d, f] = (row_id((x + d) % NX, zl, k if f == 0 else 1 - k), q)
    ydev = [None] + [(p, zh * NY + (y + d) % NY) for d in range(1, NY)]
    zpos = [(z + d) % NZ for d in range(NZ)]
    zdev = [None] + [(row_id(x, zpos[d] % NZL, k), (zpos[d] // NZL) * NY + y) for d in range(1, NZ)]

    barrier = pltpu.get_barrier_semaphore()
    for dev in list(xk.values()) + ydev[1:] + zdev[1:]:
        pl.semaphore_signal(barrier, inc=1, device_id=dev, device_id_type=MESH)
    pl.semaphore_wait(barrier, 7 + NY - 1 + NZ - 1)

    core = rcopy(aue_ref.at[1 - k], kbuf, ks.at[0], kr.at[0], xk[0, 1])
    core.start()
    ycopies = []
    for d in (1, 7, 2, 6, 3, 5, 4):
        copy = rcopy(
            yz_ref.at[:, (y + d) % NY], yzbuf.at[d - 1], vs.at[d - 1], vr.at[d - 1], ydev[d]
        )
        copy.start()
        ycopies.append(copy)

    core.wait_recv()
    acc[...] = aue_ref[k] + kbuf[...]
    busy = x < 3

    def xsend(d):
        m = (x + d) % NX
        return m, lambda: rcopy(
            acc.at[m], xbuf.at[d - 1], xs.at[d - 1], xr.at[d - 1], xk[d, 0]
        )

    for d in (2, 1, 3):
        m, make = xsend(d)

        @pl.when(m < 3)
        def _():
            make().start()

    @pl.when(busy)
    def _():
        for d in range(1, NX):
            got = xbuf.at[d - 1]
            rcopy(got, got, xs.at[d - 1], xr.at[d - 1], xk[d, 0]).wait_recv()
        total = (acc[x] + xbuf[0]) + (xbuf[1] + xbuf[2])
        accx[...] = total.reshape(NZH, NY, SHARE, 128)
        for d in range(1, NY):
            rcopy(
                accx.at[:, (y + d) % NY], ybuf.at[d - 1], ys.at[d - 1], yr.at[d - 1], ydev[d]
            ).start()
        for d in range(1, NY):
            got = ybuf.at[d - 1]
            rcopy(got, got, ys.at[d - 1], yr.at[d - 1], ydev[d]).wait_recv()
        total = accx[:, y]
        for d in range(NY - 1):
            total = total + ybuf[d]
        accy[...] = total
        for d in range(1, NZ):
            rcopy(
                accy.at[zpos[d] // NZL], zbuf.at[d - 1], zs.at[d - 1], zr.at[d - 1], zdev[d]
            ).start()

    for copy in ycopies:
        copy.wait_recv()
    total = yz_ref[:, y]
    for d in range(NY - 1):
        total = total + yzbuf[d]
    yzacc[...] = total
    hop = rcopy(yzacc.at[1 - zh], hbuf, hs.at[0], hr.at[0], zdev[NZL])
    hop.start()

    def fsend(d, f):
        n = d * 2 + f - 1
        return rcopy(auo.at[x, k], auo.at[x, k], fs.at[n], fr.at[n], xk[d, f])

    @pl.when(busy)
    def _():
        for d in range(1, NZ):
            got = zbuf.at[d - 1]
            rcopy(got, got, zs.at[d - 1], zr.at[d - 1], zdev[d]).wait_recv()
        total = accy[zh]
        for d in range(NZ - 1):
            total = total + zbuf[d]
        auo[x, k] = total
        for d, f in xk:
            fsend(d, f).start()

    hop.wait_recv()
    yzo[...] = yzacc[zh] + hbuf[...]

    for d, f in xk:
        m = (x + NX - d) % NX
        n = d * 2 + f - 1

        @pl.when(m < 3)
        def _():
            got = auo.at[m, k if f == 0 else 1 - k]
            rcopy(got, got, fs.at[n], fr.at[n], xk[d, f]).wait_recv()

    core.wait_send()
    hop.wait_send()
    for copy in ycopies:
        copy.wait_send()
    for d in (2, 1, 3):
        m, make = xsend(d)

        @pl.when(m < 3)
        def _():
            make().wait_send()

    @pl.when(busy)
    def _():
        for d in range(1, NY):
            rcopy(
                accx.at[:, (y + d) % NY], ybuf.at[d - 1], ys.at[d - 1], yr.at[d - 1], ydev[d]
            ).wait_send()
        for d in range(1, NZ):
            rcopy(
                accy.at[zpos[d] // NZL], zbuf.at[d - 1], zs.at[d - 1], zr.at[d - 1], zdev[d]
            ).wait_send()
        for d, f in xk:
            fsend(d, f).wait_send()


def gather(yz, aue):
    vmem = pl.BlockSpec(memory_space=pltpu.VMEM)
    dma = pltpu.SemaphoreType.DMA
    rows = SL * CB
    return pl.pallas_call(
        gather_kernel,
        out_shape=(
            jax.ShapeDtypeStruct((rows, 2 * W), F32),
            jax.ShapeDtypeStruct((3, 2, SHARE, 128), F32),
        ),
        in_specs=[vmem, vmem],
        out_specs=(vmem, vmem),
        scratch_shapes=[
            pltpu.VMEM((3, W, 128), F32),
            pltpu.VMEM((3, W, 128), F32),
            pltpu.VMEM((3, W, 128), F32),
            pltpu.VMEM((NZH, NY, SHARE, 128), F32),
            pltpu.VMEM((NY - 1, NZH, SHARE, 128), F32),
            pltpu.VMEM((NZH, SHARE, 128), F32),
            pltpu.VMEM((NZ - 1, SHARE, 128), F32),
            pltpu.VMEM((NY - 1, NZH, rows, 2 * W), F32),
            pltpu.VMEM((NZH, rows, 2 * W), F32),
            pltpu.VMEM((rows, 2 * W), F32),
            dma((1,)), dma((1,)),
            dma((3,)), dma((3,)),
            dma((7,)), dma((7,)),
            dma((7,)), dma((7,)),
            dma((7,)), dma((7,)),
            dma((7,)), dma((7,)),
            dma((1,)), dma((1,)),
        ],
        compiler_params=pltpu.CompilerParams(collective_id=1, has_side_effects=True),
        name="gather",
    )(yz, aue)


def body(
    cached_inverse,
    parent_panel,
    parent_blocks,
    parent_sizes,
    parent_diagonal,
    child_panel,
    child_top,
    child_blocks,
    child_sizes,
    child_diagonal,
):
    row_index = lax.axis_index("row")
    col_index = lax.axis_index("col")
    lane = jnp.arange(B, dtype=jnp.int32)[None, :]
    parent_live = lane < parent_sizes[:, None]
    child_live = lane < child_sizes[:, None]
    parent_own = jnp.where(parent_live[None], parent_panel, 0.0).reshape(SHARE, ROWS)
    child_own = jnp.where(child_live[None], child_panel, 0.0).reshape(SHARE, ROWS)
    local = jnp.maximum(parent_blocks, 0) // NROW
    tags = jnp.broadcast_to(jnp.pad(local.astype(F32), (0, 128 - SL))[None], (SHARE, 128))
    pieces = jnp.concatenate([child_top, parent_own, child_own, tags], axis=1)
    patch, own = spread(pieces)
    heard = patch[:: NCOL, 0, 2 * ROWS : 2 * ROWS + SL].astype(jnp.int32)
    columns = heard * 2 + jnp.arange(2, dtype=jnp.int32)[:, None]
    idx = jnp.concatenate([
        local,
        columns.reshape(-1),
        parent_sizes,
        child_sizes,
        jnp.stack([col_index * SHARE, (row_index == 0).astype(jnp.int32)]),
    ])
    yz, aue = multiply(
        idx,
        cached_inverse.reshape(RC * B * 8, B),
        patch.reshape(2, W, PATCH),
        own.reshape(W, OWN),
        parent_diagonal,
    )
    rows, mats = gather(yz.reshape(NZH, NY, SL * CB, 2 * W), aue)
    put = (parent_blocks[None, :] == (jnp.arange(RC, dtype=jnp.int32) * NROW + row_index)[:, None])
    rows = rows.reshape(SL, CB, 2 * W)
    laid = sum(jnp.where(put[:, s][:, None, None], rows[s][None], 0.0) for s in range(SL))
    mats = jnp.transpose(mats, (0, 2, 1, 3)).reshape(3, SHARE, W)
    return (
        laid[:, None, :, 0:W],
        parent_diagonal - mats[0],
        laid[:, None, :, W:],
        mats[1],
        child_diagonal + mats[2],
    )


def solution(mesh):
    in_specs = (
        P(None, "row", None, None, "col", None),
        P("col", "row", None),
        P("row"),
        P("row"),
        P("col", None),
        P("col", "row", None),
        P("col", None),
        P("row"),
        P("row"),
        P("col", None),
    )
    out_specs = (
        P(None, "row", "col", None),
        P("col", None),
        P(None, "row", "col", None),
        P("col", None),
        P("col", None),
    )
    return jax.shard_map(body, mesh=mesh, in_specs=in_specs, out_specs=out_specs, check_vma=False)
```

time: 1200 us -> 98.9 us (0.08)
  waiting for transfers between devices: 957 us -> 0 us
  blocking collectives: 170 us -> 0 us
  Pallas kernels: 0 us -> 87.1 us
  matrix products: 24.9 us -> 0 us
  between operations: 14.6 us -> 0.69 us
  local copies, waits for them, and re-layouts: 17 us -> 4.24 us
    psum x3 -> x0, waiting for transfers between devices: 823 us -> none  [the longest x2 550 us: diagonal_sum(): entire = lax.psum(partial_rows(0, panel_width), ('row', 'col'))]
    all_gather x3 -> x0, blocking collectives: 145 us -> none  [the longest x1 54.9 us: body(): wide_parent = lax.all_gather(parent_panel, 'col', axis=0, tiled=True)]
    unnamed x5 -> x0, waiting for transfers between devices: 133 us -> none
    pallas_call x0 -> x3, Pallas kernels: none -> 87.1 us  [the longest x1 41.3 us: spread(): pl.pallas_call(spread_kernel, out_shape=(jax.ShapeDtypeStruct((NROW, SHAR...]
    psum x1 -> x0, blocking collectives: 25.1 us -> none  [from_root(): return lax.psum(kept, axis)]
    dot_general x16 -> x0, matrix products: 24.9 us -> none  [the longest x4 6.68 us: add_columns(): jnp.einsum('ck,wky->cwy', onehot, widened, precision=highest)]
  transfers between devices with their start and end apart: 4 -> 0, of which waited for: 4 -> 0; matrix products, arithmetic and copies ran while one was open for 1% -> 0% of each run, Pallas kernels for 0% -> 0%
where the time goes in v1:
time: 98.9 us; the launch traced here: 98.4 us
  Pallas kernels  87.1 us (88%)
  other arithmetic  6.35 us (6%)
  local copies, waits for them, and re-layouts  4.24 us (4%)
    pallas_call x1, Pallas kernels, spread(): pl.pallas_call(spread_kernel, out_shape=(jax.ShapeDtypeStruct((NROW, SHAR...  41.3 us
    pallas_call x1, Pallas kernels, gather(): pl.pallas_call(gather_kernel, out_shape=(jax.ShapeDtypeStruct((rows, 2 *...  39.1 us
    pallas_call x1, Pallas kernels, multiply(): pl.pallas_call(multiply_kernel, out_shape=(jax.ShapeDtypeStruct((NCOL, SL...  6.72 us

profile of v1, /device:TPU:1, one launch (start us, length us, event | category | flops | bytes accessed | tf_op | source)
XLA Modules:
  0.0 98.4 jit_solution(6579349946150137651)
XLA Ops:
  0.6 0.7 iota_compare_fusion.1
  1.4 0.7 iota_compare_fusion.2
  2.1 0.8 copy_bitcast_fusion
  2.8 0.7 fusion
  3.5 1.4 %maximum_maximum_fusion.x_ref = f32[16,1152]{1,0:T(8,128)} fusion(f32[16,384]{1,0:T(8,128)S(1)} %get-tuple-element.30, f32[16,384]{1,0:T(8,128)S(1)} %get-tuple-element.31, f32[16,256]{1,0:T(8,128)} %param.16, f32[1152]{0:T(1024)S(1)} %pad_select_fusion), kind=kLoop, calls=%fused_computation | loop fusion | flops 55296 | bytes 143872 | tf_op jit(solution)/shard_map/concatenate | solution.py:480
  4.9 41.3 %spread.1 = (f32[32,16,896]{2,1,0:T(8,128)}, f32[16,16,1024]{2,1,0:T(8,128)}) custom-call(f32[16,1152]{1,0:T(8,128)} %maximum_maximum_fusion.x_ref), custom_call_target="tpu_custom_call" | custom-call | tf_op jit(solution)/shard_map/spread/pallas_call | solution.py:193
  46.2 0.7 multiply_reduce_fusion
  46.9 0.1 mul.19
  47.0 0.1 add.36
  47.1 1.3 %concatenate.7.idx = s32[17]{0:T(128)} concatenate(s32[3]{0:T(128)S(1)} %get-tuple-element.18, s32[6]{0:T(128)S(1)} %add.37, s32[3]{0:T(128)} %param.13, s32[3]{0:T(128)} %param.17, s32[1]{0:T(128)} %bitcast.1, s32[1]{0:T(128)} %bitcast.2), dimensions={0} | concatenate | bytes 136 | tf_op jit(solution)/shard_map/concatenate | solution.py:484
  48.4 0.0 copy-start.2
  48.4 6.7 %multiply.1 = (f32[16,24,512]{2,1,0:T(8,128)}, f32[2,3,256,128]{3,2,1,0:T(8,128)}) custom-call(s32[17]{0:T(128)} %concatenate.7.idx, f32[4096,128]{1,0:T(8,128)} %bitcast.40, f32[2,256,896]{2,1,0:T(8,128)} %bitcast.41, f32[256,1024]{1,0:T(8,128)} %bitcast.42, f32[16,256]{1,0:T(8,128)} %d_ref.1), custom_call_target="tpu_custom_call" | custom-call | tf_op jit(solution)/shard_map/multiply/pallas_call | solution.py:272
  55.1 0.0 copy-start.1
  55.1 0.0 copy-start
  55.1 39.1 %gather.1 = (f32[24,512]{1,0:T(8,128)}, f32[3,2,16,128]{3,2,1,0:T(8,128)}) custom-call(f32[2,8,24,512]{3,2,1,0:T(8,128)} %bitcast.43, f32[2,3,256,128]{3,2,1,0:T(8,128)} %get-tuple-element.14.aue_ref), custom_call_target="tpu_custom_call" | custom-call | tf_op jit(solution)/shard_map/gather/pallas_call | solution.py:427
  94.2 0.8 fusion.2
  94.9 0.0 copy-done.2
  94.9 0.1 broadcast_compare_fusion
  95.0 0.1 select_add_fusion
  95.1 0.6 slice_bitcast_fusion
  95.8 0.8 fusion.1
  96.5 0.6 copy.31
  97.1 0.0 copy-done.1
  97.1 0.6 bitcast_add_fusion
  97.8 0.0 copy-done
  97.8 0.6 bitcast_subtract_fusion
  (8 shorter events, 0.1 us)
Async XLA Ops:
  48.4 46.6 %copy-start.2 = (s32[3]{0:T(128)S(1)}, s32[3]{0:T(128)}, u32[]{:S(2)}) copy-start(s32[3]{0:T(128)} %param.12) | copy-start | bytes 40
  55.1 42.1 %copy-start.1 = (f32[16,256]{1,0:T(8,128)S(1)}, f32[16,256]{1,0:T(8,128)}, u32[]{:S(2)}) copy-start(f32[16,256]{1,0:T(8,128)} %param.18) | copy-start | bytes 49156
  55.1 42.7 %copy-start = (f32[16,256]{1,0:T(8,128)S(1)}, f32[16,256]{1,0:T(8,128)}, u32[]{:S(2)}) copy-start(f32[16,256]{1,0:T(8,128)} %d_ref.1) | copy-start | bytes 49156

commit v2 on v0

v2 whole, which is shorter than its diff:
```python
import jax
import jax.numpy as jnp
from jax import lax
from jax.experimental import pallas as pl
from jax.experimental.pallas import tpu as pltpu
from jax.sharding import PartitionSpec as P

MESH = pl.DeviceIdType.MESH
F32 = jnp.float32
BF16 = jnp.bfloat16

NX, NZL, NZH, NY, NK = 4, 4, 2, 8, 2
NZ = NZL * NZH
NROW, NCOL = NX * NZL * NK, NZH * NY
W, B, SL, RC = 256, 128, 3, 4
SHARE = W // NCOL
ROWS = SL * B
CB = B // NCOL
PATCH = 2 * ROWS + 128
OWN = W + 2 * ROWS
WIDE = W + PATCH
UPS = (4, 3)
DOWNS = (3, 4)


def place():
    p = lax.axis_index("row")
    q = lax.axis_index("col")
    x = p // (NZL * NK)
    zl = (p // NK) % NZL
    k = p % NK
    return p, q, x, zl, k, q // NY, q % NY


def row_id(x, zl, k):
    return (x * NZL + zl) * NK + k


def rcopy(src, dst, send, recv, target):
    return pltpu.make_async_remote_copy(
        src_ref=src,
        dst_ref=dst,
        send_sem=send,
        recv_sem=recv,
        device_id=target,
        device_id_type=MESH,
    )


def halves(a):
    hi = a.astype(BF16)
    lo = (a - hi.astype(F32)).astype(BF16)
    return hi, lo


def dot3(a, b, dims):
    def one(u, v):
        return lax.dot_general(u, v, (dims, ((), ())), preferred_element_type=F32)

    return one(a[0], b[0]) + (one(a[0], b[1]) + one(a[1], b[0]))


NN = ((1,), (0,))
NT = ((1,), (1,))


def pick(values, which, first=0):
    out = values[0]
    for n in range(1, len(values)):
        out = jnp.where(which == n, values[n], out)
    return out


def step_kernel(
    pb, psz, csz, s_hbm, pp_ref, cp_ref, top_ref, d_ref,
    yzo, auo,
    sv, sub8, sub, xv, g_ref, c_ref, yv, zv, uv, yz, aue,
    kbuf, acc, xbuf, accx, ybuf, accy, zbuf, ubuf, dbuf, yzacc, hbuf,
    ssem, ps, pr, lsem, gzs, gzr, gxs, gxr, gks, gkr, chs, chr_, cus, cur, cds, cdr,
    ks, kr, xs, xr, ys, yr, zs, zr, fs, fr, us, ur, ds, dr, hs, hr,
):
    p, q, x, zl, k, zh, y = place()
    z = zh * NZL + zl
    half, cls = p // NCOL, p % NCOL
    fixed = q == cls
    swap = (half * NCOL + q, cls)
    xk = {}
    for d in range(NX):
        for f in range(2):
            if d or f:
                xk[d, f] = (row_id((x + d) % NX, zl, k if f == 0 else 1 - k), q)
    core = xk[0, 1]
    lzdev = [None] + [(row_id(x, (zl + d) % NZL, k), q) for d in range(1, NZL)]
    ydev = [None] + [(p, zh * NY + (y + d) % NY) for d in range(1, NY)]
    up, down = ydev[1], ydev[NY - 1]
    zpos = [(z + d) % NZ for d in range(NZ)]
    zdev = [None] + [(row_id(x, zpos[d] % NZL, k), (zpos[d] // NZL) * NY + y) for d in range(1, NZ)]
    far = zdev[NZL]

    load_s = pltpu.make_async_copy(s_hbm, sv, ssem.at[0])
    load_s.start()

    barrier = pltpu.get_barrier_semaphore()

    @pl.when(jnp.logical_not(fixed))
    def _():
        pl.semaphore_signal(barrier, inc=1, device_id=swap, device_id_type=MESH)

    for dev in zdev[1:] + ydev[1:] + list(xk.values()):
        pl.semaphore_signal(barrier, inc=1, device_id=dev, device_id_type=MESH)

    lane = lax.broadcasted_iota(jnp.int32, (SHARE, B), 1)
    xv[:, 0:W] = top_ref[...]
    for s in range(SL):
        at = W + s * B
        xv[:, at : at + B] = jnp.where(lane < psz[s], pp_ref[s], 0.0)
        at += ROWS
        xv[:, at : at + B] = jnp.where(lane < csz[s], cp_ref[s], 0.0)
    local = [jnp.maximum(pb[s], 0) // NROW for s in range(SL)]
    tag = jnp.zeros((SHARE, 128), F32)
    tags = lax.broadcasted_iota(jnp.int32, (SHARE, 128), 1)
    for s in range(SL):
        tag = jnp.where(tags == s, local[s].astype(F32), tag)
    xv[:, OWN:WIDE] = tag
    c_ref[q] = xv[:, 0:OWN]

    pl.semaphore_wait(barrier, 7 + NY - 1 + NZ - 1 + jnp.where(fixed, 0, 1))

    sends = []

    def send(*args):
        copy = rcopy(*args)
        copy.start()
        sends.append(copy)

    piece = xv.at[:, W:WIDE]
    mine = xv.at[:, 0:OWN]
    out = rcopy(piece, g_ref.at[half * NCOL + q], ps.at[0], pr.at[0], swap)
    keep = pltpu.make_async_copy(piece, g_ref.at[p], lsem.at[0])

    @pl.when(jnp.logical_not(fixed))
    def _():
        out.start()

    @pl.when(fixed)
    def _():
        keep.start()

    def ring(a, t, src_up, src_down):
        zz = zh if a == 0 else 1 - zh
        if src_up is not None:
            at = zz * NY + (y + NY - t) % NY
            send(src_up, c_ref.at[at], cus.at[a * 4 + t], cur.at[a * 4 + t], up)
        if src_down is not None:
            at = zz * NY + (y + t) % NY
            send(src_down, c_ref.at[at], cds.at[a * 4 + t], cdr.at[a * 4 + t], down)

    def ring_up_wait(a, t):
        zz = zh if a == 0 else 1 - zh
        got = c_ref.at[zz * NY + (y + NY - 1 - t) % NY]
        rcopy(got, got, cus.at[a * 4 + t], cur.at[a * 4 + t], up).wait_recv()
        if t + 1 < UPS[a]:
            ring(a, t + 1, got, None)

    def ring_down_wait(a, t):
        zz = zh if a == 0 else 1 - zh
        got = c_ref.at[zz * NY + (y + 1 + t) % NY]
        rcopy(got, got, cds.at[a * 4 + t], cdr.at[a * 4 + t], down).wait_recv()
        if t + 1 < DOWNS[a]:
            ring(a, t + 1, None, got)

    send(mine, c_ref.at[q], chs.at[0], chr_.at[0], far)
    ring(0, 0, mine, mine)

    load_s.wait()
    for s in range(SL):
        for c in range(8):
            blocks = [sv[pl.ds(r * B * 8 + c, B, stride=8), :] for r in range(RC)]
            sub8[s * B : (s + 1) * B, c * B : (c + 1) * B] = pick(blocks, local[s])

    ring_up_wait(0, 0)
    ring_down_wait(0, 0)
    other = c_ref.at[(1 - zh) * NY + y]
    rcopy(other, other, chs.at[0], chr_.at[0], far).wait_recv()
    ring(1, 0, other, other)

    @pl.when(jnp.logical_not(fixed))
    def _():
        rcopy(piece, g_ref.at[p], ps.at[0], pr.at[0], swap).wait_recv()

    @pl.when(fixed)
    def _():
        keep.wait()

    def fan(src, dz):
        got = g_ref.at[src]
        for d in (1, 3):
            send(got, got, gxs.at[dz * 3 + d - 1], gxr.at[dz * 3 + d - 1], xk[d, 0])
        send(got, got, gks.at[dz * 4], gkr.at[dz * 4], core)

    own = g_ref.at[p]
    for d in (1, 3, 2):
        send(own, own, gzs.at[d - 1], gzr.at[d - 1], lzdev[d])
    fan(p, 0)

    def z_wait(d):
        src = row_id(x, (zl + NZL - d) % NZL, k)
        got = g_ref.at[src]
        rcopy(got, got, gzs.at[d - 1], gzr.at[d - 1], lzdev[d]).wait_recv()
        fan(src, d)

    def x_wait(dz, d):
        src = row_id((x + NX - d) % NX, (zl + NZL - dz) % NZL, k)
        got = g_ref.at[src]
        n = dz * 3 + d - 1
        rcopy(got, got, gxs.at[n], gxr.at[n], xk[d, 0]).wait_recv()
        n = dz * 3 + 1
        if d == (1 if dz % 2 == 0 else 3):
            send(got, got, gxs.at[n], gxr.at[n], xk[d, 0])
        send(got, got, gks.at[dz * 4 + d], gkr.at[dz * 4 + d], core)

    ring_up_wait(0, 1)
    ring_down_wait(0, 1)
    ring_up_wait(1, 0)
    ring_down_wait(1, 0)
    z_wait(1)
    z_wait(3)
    x_wait(0, 1)
    x_wait(0, 3)
    ring_up_wait(0, 2)
    ring_up_wait(1, 1)
    ring_down_wait(1, 1)
    z_wait(2)
    x_wait(1, 1)
    x_wait(1, 3)
    x_wait(3, 1)
    x_wait(3, 3)
    ring_down_wait(0, 2)
    ring_up_wait(0, 3)
    ring_up_wait(1, 2)
    ring_down_wait(1, 2)
    x_wait(0, 2)
    x_wait(2, 1)
    x_wait(2, 3)
    x_wait(1, 2)
    x_wait(3, 2)
    ring_down_wait(1, 3)
    x_wait(2, 2)
    for dz in (0, 1, 3, 2):
        for d in (0, 1, 3, 2):
            src = row_id((x + NX - d) % NX, (zl + NZL - dz) % NZL, 1 - k)
            got = g_ref.at[src]
            rcopy(got, got, gks.at[dz * 4 + d], gkr.at[dz * 4 + d], core).wait_recv()

    for h in range(2):
        heard = g_ref[h * NCOL, 0:8, 2 * ROWS : 2 * ROWS + 128]
        for t in range(SL):
            which = jnp.max(jnp.where(tags[0:8] == t, heard, 0.0))
            for s in range(SL):
                at = slice(s * B, (s + 1) * B)
                blocks = [sub8[at, (2 * r + h) * B : (2 * r + h + 1) * B] for r in range(RC)]
                n = h * SL + t
                value = blocks[0]
                for r in range(1, RC):
                    value = jnp.where(which > r - 0.5, blocks[r], value)
                sub[at, n * B : (n + 1) * B] = value

    def panel(h, at):
        return halves(g_ref[h * NCOL : (h + 1) * NCOL, :, at : at + ROWS].reshape(W, ROWS))

    gp = [panel(h, 0) for h in range(2)]
    gq = [panel(h, ROWS) for h in range(2)]
    topf = c_ref[:, :, 0:W].reshape(W, W)
    top = halves(topf)
    rows = lax.broadcasted_iota(jnp.int32, (B, 1), 0)
    for s in range(SL):
        at = slice(s * B, (s + 1) * B)
        left = [halves(sub[at, h * ROWS : (h + 1) * ROWS]) for h in range(2)]
        yp = dot3(left[0], gp[0], NT) + dot3(left[1], gp[1], NT)
        yy = jnp.where(rows < psz[s], -yp, 0.0)
        zq = dot3(left[0], gq[0], NT) + dot3(left[1], gq[1], NT)
        zz = jnp.where(rows < csz[s], -(zq + dot3(halves(yy), top, NN)), 0.0)
        yv[at, :] = yy
        zv[at, :] = zz
        yz[:, :, s * CB : (s + 1) * CB, 0:W] = yy.reshape(NZH, NY, CB, W)
        yz[:, :, s * CB : (s + 1) * CB, W : 2 * W] = zz.reshape(NZH, NY, CB, W)

    def sum_up(a, t):
        n = a * 4 + t
        dst = ubuf.at[n]
        if t == 0:
            src = yz.at[a, (y + UPS[a]) % NY]
        else:
            src = ubuf.at[n - 1]
            rcopy(src, src, us.at[n - 1], ur.at[n - 1], up).wait_recv()
            ubuf[n - 1] = ubuf[n - 1] + yz[a, (y + UPS[a] - t) % NY]
        send(src, dst, us.at[n], ur.at[n], up)

    def sum_down(a, t):
        n = a * 4 + t
        dst = dbuf.at[n]
        if t == 0:
            src = yz.at[a, (y + NY - DOWNS[a]) % NY]
        else:
            src = dbuf.at[n - 1]
            rcopy(src, src, ds.at[n - 1], dr.at[n - 1], down).wait_recv()
            dbuf[n - 1] = dbuf[n - 1] + yz[a, (y + NY - DOWNS[a] + t) % NY]
        send(src, dst, ds.at[n], dr.at[n], down)

    def sum_step(t):
        for a in range(2):
            if t < UPS[a]:
                sum_up(a, t)
            if t < DOWNS[a]:
                sum_down(a, t)

    sum_step(0)

    def put(m, mat):
        for n in range(2):
            aue[n, m] = mat[:, n * 128 : (n + 1) * 128]
        send(aue.at[1 - k, m], kbuf.at[m], ks.at[m], kr.at[m], core)

    pp = halves(c_ref[:, :, W : W + ROWS].reshape(W, ROWS))
    qp = halves(c_ref[:, :, W + ROWS : OWN].reshape(W, ROWS))
    ysp = halves(yv[...])
    a_mat = dot3(pp, ysp, NN)
    put(0, a_mat)
    uv[...] = dot3(halves(a_mat), top, NN) - dot3(qp, ysp, NN).T
    first = jnp.where(p == 0, 1.0, 0.0)
    mid = pl.ds(pl.multiple_of(q * SHARE, SHARE), SHARE)
    uv[mid, :] = uv[mid, :] - first * dot3(halves(d_ref[...]), top, NN)
    u_mat = uv[...]
    put(1, u_mat)
    sum_step(1)
    e_mat = -dot3(halves(topf.T), halves(u_mat), NN) - dot3(qp, halves(zv[...]), NN)
    put(2, e_mat)
    sum_step(2)

    busy = x < 3

    def xcopy(m, d):
        return rcopy(acc.at[m], xbuf.at[d - 1], xs.at[d - 1], xr.at[d - 1], xk[d, 0])

    for m in range(3):
        got = kbuf.at[m]
        rcopy(got, got, ks.at[m], kr.at[m], core).wait_recv()
        acc[m] = aue[k, m] + kbuf[m]
    for d in (2, 1, 3):
        m = (x + d) % NX

        @pl.when(m < 3)
        def _():
            xcopy(m, d).start()

    sum_step(3)

    for a in range(2):
        n = a * 4 + UPS[a] - 1
        got = ubuf.at[n]
        rcopy(got, got, us.at[n], ur.at[n], up).wait_recv()
        n2 = a * 4 + DOWNS[a] - 1
        got = dbuf.at[n2]
        rcopy(got, got, ds.at[n2], dr.at[n2], down).wait_recv()
        yzacc[a] = yz[a, y] + (ubuf[n] + dbuf[n2])
    send(yzacc.at[1 - zh], hbuf, hs.at[0], hr.at[0], far)

    def ycopy(d):
        return rcopy(accx.at[:, (y + d) % NY], ybuf.at[d - 1], ys.at[d - 1], yr.at[d - 1], ydev[d])

    def zcopy(d):
        return rcopy(accy.at[zpos[d] // NZL], zbuf.at[d - 1], zs.at[d - 1], zr.at[d - 1], zdev[d])

    def fcopy(d, f):
        n = d * 2 + f - 1
        return rcopy(auo.at[x, k], auo.at[x, k], fs.at[n], fr.at[n], xk[d, f])

    @pl.when(busy)
    def _():
        for d in range(1, NX):
            xcopy(x, d).wait_recv()
        total = (acc[x] + xbuf[0]) + (xbuf[1] + xbuf[2])
        accx[...] = total.reshape(NZH, NY, SHARE, 128)
        for d in (4, 3, 5, 2, 6, 1, 7):
            ycopy(d).start()

    hop = rcopy(hbuf, hbuf, hs.at[0], hr.at[0], far)
    hop.wait_recv()
    yzo[...] = yzacc[zh] + hbuf[...]

    @pl.when(busy)
    def _():
        for d in range(1, NY):
            ycopy(d).wait_recv()
        total = accx[:, y]
        for d in range(NY - 1):
            total = total + ybuf[d]
        accy[...] = total
        for d in (4, 3, 5, 2, 6, 1, 7):
            zcopy(d).start()
        for d in range(1, NZ):
            zcopy(d).wait_recv()
        total = accy[zh]
        for d in range(NZ - 1):
            total = total + zbuf[d]
        auo[x, k] = total
        for d, f in xk:
            fcopy(d, f).start()

    for d, f in xk:
        m = (x + NX - d) % NX
        n = d * 2 + f - 1

        @pl.when(m < 3)
        def _():
            got = auo.at[m, k if f == 0 else 1 - k]
            rcopy(got, got, fs.at[n], fr.at[n], xk[d, f]).wait_recv()

    @pl.when(jnp.logical_not(fixed))
    def _():
        out.wait_send()

    for copy in sends:
        copy.wait_send()
    for d in (2, 1, 3):
        m = (x + d) % NX

        @pl.when(m < 3)
        def _():
            xcopy(m, d).wait_send()

    @pl.when(busy)
    def _():
        for d in range(1, NY):
            ycopy(d).wait_send()
        for d in range(1, NZ):
            zcopy(d).wait_send()
        for d, f in xk:
            fcopy(d, f).wait_send()


def step(*operands):
    vmem = pl.BlockSpec(memory_space=pltpu.VMEM)
    smem = pl.BlockSpec(memory_space=pltpu.SMEM)
    dma = pltpu.SemaphoreType.DMA
    rows = SL * CB
    buffers = [
        (RC * B * 8, B),
        (ROWS, 8 * B),
        (ROWS, 2 * ROWS),
        (SHARE, WIDE),
        (NROW, SHARE, PATCH),
        (NCOL, SHARE, OWN),
        (ROWS, W),
        (ROWS, W),
        (W, W),
        (NZH, NY, rows, 2 * W),
        (2, 3, W, 128),
        (3, W, 128),
        (3, W, 128),
        (3, W, 128),
        (NZH, NY, SHARE, 128),
        (NY - 1, NZH, SHARE, 128),
        (NZH, SHARE, 128),
        (NZ - 1, SHARE, 128),
        (8, rows, 2 * W),
        (8, rows, 2 * W),
        (NZH, rows, 2 * W),
        (rows, 2 * W),
    ]
    sems = [1, 1, 1, 1, 3, 3, 12, 12, 16, 16, 1, 1, 8, 8, 8, 8]
    sems += [3, 3, 3, 3, 7, 7, 7, 7, 7, 7, 8, 8, 8, 8, 1, 1]
    return pl.pallas_call(
        step_kernel,
        out_shape=(
            jax.ShapeDtypeStruct((rows, 2 * W), F32),
            jax.ShapeDtypeStruct((3, 2, SHARE, 128), F32),
        ),
        in_specs=[smem] * 3 + [pl.BlockSpec(memory_space=pl.ANY)] + [vmem] * 4,
        out_specs=(vmem, vmem),
        scratch_shapes=[pltpu.VMEM(b, F32) for b in buffers] + [dma((n,)) for n in sems],
        compiler_params=pltpu.CompilerParams(collective_id=0, has_side_effects=True),
        name="step",
    )(*operands)


def place_kernel(pb, yz_ref, mats_ref, d_ref, cd_ref, prow, pd, crow, cu, cdiag):
    p = lax.axis_index("row")
    for r in range(RC):
        ya = jnp.zeros((CB, W), F32)
        za = jnp.zeros((CB, W), F32)
        for s in range(SL):
            here = pb[s] == r * NROW + p
            ya = jnp.where(here, yz_ref[s * CB : (s + 1) * CB, 0:W], ya)
            za = jnp.where(here, yz_ref[s * CB : (s + 1) * CB, W:], za)
        prow[r] = ya
        crow[r] = za
    for n in range(2):
        at = slice(n * 128, (n + 1) * 128)
        pd[:, at] = d_ref[:, at] - mats_ref[0, n]
        cu[:, at] = mats_ref[1, n]
        cdiag[:, at] = cd_ref[:, at] + mats_ref[2, n]


def lay(*operands):
    vmem = pl.BlockSpec(memory_space=pltpu.VMEM)
    smem = pl.BlockSpec(memory_space=pltpu.SMEM)
    share = jax.ShapeDtypeStruct((SHARE, W), F32)
    rows = jax.ShapeDtypeStruct((RC, CB, W), F32)
    return pl.pallas_call(
        place_kernel,
        out_shape=(rows, share, rows, share, share),
        in_specs=[smem] + [vmem] * 4,
        out_specs=(vmem,) * 5,
        name="lay",
    )(*operands)


def body(
    cached_inverse,
    parent_panel,
    parent_blocks,
    parent_sizes,
    parent_diagonal,
    child_panel,
    child_top,
    child_blocks,
    child_sizes,
    child_diagonal,
):
    rows, mats = step(
        parent_blocks,
        parent_sizes,
        child_sizes,
        cached_inverse.reshape(RC * B * 8, B),
        jnp.transpose(parent_panel, (1, 0, 2)),
        jnp.transpose(child_panel, (1, 0, 2)),
        child_top,
        parent_diagonal,
    )
    prow, pd, crow, cu, cdiag = lay(parent_blocks, rows, mats, parent_diagonal, child_diagonal)
    return (prow[:, None], pd, crow[:, None], cu, cdiag)


def solution(mesh):
    in_specs = (
        P(None, "row", None, None, "col", None),
        P("col", "row", None),
        P("row"),
        P("row"),
        P("col", None),
        P("col", "row", None),
        P("col", None),
        P("row"),
        P("row"),
        P("col", None),
    )
    out_specs = (
        P(None, "row", "col", None),
        P("col", None),
        P(None, "row", "col", None),
        P("col", None),
        P("col", None),
    )
    return jax.shard_map(body, mesh=mesh, in_specs=in_specs, out_specs=out_specs, check_vma=False)
```

time: 1200 us -> 78.7 us (0.07)
  waiting for transfers between devices: 957 us -> 0 us
  blocking collectives: 170 us -> 0 us
  Pallas kernels: 0 us -> 77.8 us
  matrix products: 24.9 us -> 0 us
  local copies, waits for them, and re-layouts: 17 us -> 0 us
  between operations: 14.6 us -> 0.64 us
    psum x3 -> x0, waiting for transfers between devices: 823 us -> none  [the longest x2 550 us: diagonal_sum(): entire = lax.psum(partial_rows(0, panel_width), ('row', 'col'))]
    all_gather x3 -> x0, blocking collectives: 145 us -> none  [the longest x1 54.9 us: body(): wide_parent = lax.all_gather(parent_panel, 'col', axis=0, tiled=True)]
    unnamed x5 -> x0, waiting for transfers between devices: 133 us -> none
    pallas_call x0 -> x2, Pallas kernels: none -> 77.8 us  [the longest x1 76.3 us: step(): pl.pallas_call(step_kernel, out_shape=(jax.ShapeDtypeStruct((rows, 2 * W)...]
    psum x1 -> x0, blocking collectives: 25.1 us -> none  [from_root(): return lax.psum(kept, axis)]
    dot_general x16 -> x0, matrix products: 24.9 us -> none  [the longest x4 6.68 us: add_columns(): jnp.einsum('ck,wky->cwy', onehot, widened, precision=highest)]
  transfers between devices with their start and end apart: 4 -> 0, of which waited for: 4 -> 0; matrix products, arithmetic and copies ran while one was open for 1% -> 0% of each run, Pallas kernels for 0% -> 0%
where the time goes in v2:
time: 78.7 us; the launch traced here: 78.4 us
  Pallas kernels  77.8 us (99%)
    pallas_call x1, Pallas kernels, step(): pl.pallas_call(step_kernel, out_shape=(jax.ShapeDtypeStruct((rows, 2 * W)...  76.3 us

profile of v2, /device:TPU:1, one launch (start us, length us, event | category | flops | bytes accessed | tf_op | source)
XLA Modules:
  0.0 78.4 jit_solution(9644321737885707927)
XLA Ops:
  0.6 76.3 %step.1 = (f32[24,512]{1,0:T(8,128)}, f32[3,2,16,128]{3,2,1,0:T(8,128)}) custom-call(s32[3]{0:T(128)} %pb.3, s32[3]{0:T(128)} %psz.1, s32[3]{0:T(128)} %csz.1, f32[4096,128]{1,0:T(8,128)} %bitcast.9, f32[3,16,128]{2,1,0:T(8,128)} %bitcast.10, f32[3,16,128]{2,1,0:T(8,128)} %bitcast.11, f32[16,256]{1,0:T(8,128)} %top_ref.1, f32[16,256]{1,0:T(8,128)} %d_ref.3), custom_call_target="tpu_custom_call" | custom-call | tf_op jit(solution)/shard_map/step/pallas_call | solution.py:473
  76.9 1.5 %lay.1 = (f32[4,8,256]{2,1,0:T(8,128)}, f32[16,256]{1,0:T(8,128)}, f32[4,8,256]{2,1,0:T(8,128)}, f32[16,256]{1,0:T(8,128)}, f32[16,256]{1,0:T(8,128)}) custom-call(s32[3]{0:T(128)} %pb.3, f32[24,512]{1,0:T(8,128)} %get-tuple-element.12.yz_ref, f32[3,2,16,128]{3,2,1,0:T(8,128)} %get-tuple-element.13.mats_ref, f32[16,256]{1,0:T(8,128)} %d_ref.3, f32[16,256]{1,0:T(8,128)} %cd_ref.1), custom_call_target="tpu_custom_call" | custom-call | tf_op jit(solution)/shard_map/lay/pallas_call | solution.py:510

commit v3 on v2

--- a/solution.py
+++ b/solution.py
@@ -178,8 +178,14 @@
             blocks = [sv[pl.ds(r * B * 8 + c, B, stride=8), :] for r in range(RC)]
             sub8[s * B : (s + 1) * B, c * B : (c + 1) * B] = pick(blocks, local[s])
 
-    ring_up_wait(0, 0)
-    ring_down_wait(0, 0)
+    def ring_wait(a, t):
+        if t < UPS[a]:
+            ring_up_wait(a, t)
+        if t < DOWNS[a]:
+            ring_down_wait(a, t)
+
+    ring_wait(0, 0)
+    ring_wait(0, 1)
     other = c_ref.at[(1 - zh) * NY + y]
     rcopy(other, other, chs.at[0], chr_.at[0], far).wait_recv()
     ring(1, 0, other, other)
@@ -194,7 +200,7 @@
 
     def fan(src, dz):
         got = g_ref.at[src]
-        for d in (1, 3):
+        for d in (1, 3) if dz == 0 else (2, 1, 3):
             send(got, got, gxs.at[dz * 3 + d - 1], gxr.at[dz * 3 + d - 1], xk[d, 0])
         send(got, got, gks.at[dz * 4], gkr.at[dz * 4], core)
 
@@ -215,71 +221,72 @@
         n = dz * 3 + d - 1
         rcopy(got, got, gxs.at[n], gxr.at[n], xk[d, 0]).wait_recv()
         n = dz * 3 + 1
-        if d == (1 if dz % 2 == 0 else 3):
+        if dz == 0 and d == 1:
             send(got, got, gxs.at[n], gxr.at[n], xk[d, 0])
         send(got, got, gks.at[dz * 4 + d], gkr.at[dz * 4 + d], core)
 
-    ring_up_wait(0, 1)
-    ring_down_wait(0, 1)
-    ring_up_wait(1, 0)
-    ring_down_wait(1, 0)
+    ring_wait(0, 2)
+    ring_wait(1, 0)
     z_wait(1)
     z_wait(3)
     x_wait(0, 1)
     x_wait(0, 3)
-    ring_up_wait(0, 2)
-    ring_up_wait(1, 1)
-    ring_down_wait(1, 1)
+    ring_wait(1, 1)
     z_wait(2)
+    x_wait(0, 2)
+    ring_wait(0, 3)
     x_wait(1, 1)
     x_wait(1, 3)
     x_wait(3, 1)
     x_wait(3, 3)
-    ring_down_wait(0, 2)
-    ring_up_wait(0, 3)
-    ring_up_wait(1, 2)
-    ring_down_wait(1, 2)
-    x_wait(0, 2)
+
+    def heard(slot):
+        tile = g_ref[slot, 0:8, 2 * ROWS : 2 * ROWS + 128]
+        return [jnp.max(jnp.where(tags[0:8] == t, tile, 0.0)) for t in range(SL)]
+
+    ours, theirs = heard(p), heard(row_id((x + 2) % NX, zl, k))
+    for h in range(2):
+        for t in range(SL):
+            which = jnp.where(half == h, ours[t], theirs[t])
+            for s in range(SL):
+                at = slice(s * B, (s + 1) * B)
+                n = h * SL + t
+                value = sub8[at, h * B : (h + 1) * B]
+                for r in range(1, RC):
+                    block = sub8[at, (2 * r + h) * B : (2 * r + h + 1) * B]
+                    value = jnp.where(which > r - 0.5, block, value)
+                sub[at, n * B : (n + 1) * B] = value
+
+    x_wait(1, 2)
+    x_wait(3, 2)
     x_wait(2, 1)
     x_wait(2, 3)
-    x_wait(1, 2)
-    x_wait(3, 2)
-    ring_down_wait(1, 3)
     x_wait(2, 2)
+    ring_wait(1, 2)
     for dz in (0, 1, 3, 2):
         for d in (0, 1, 3, 2):
             src = row_id((x + NX - d) % NX, (zl + NZL - dz) % NZL, 1 - k)
             got = g_ref.at[src]
             rcopy(got, got, gks.at[dz * 4 + d], gkr.at[dz * 4 + d], core).wait_recv()
 
-    for h in range(2):
-        heard = g_ref[h * NCOL, 0:8, 2 * ROWS : 2 * ROWS + 128]
-        for t in range(SL):
-            which = jnp.max(jnp.where(tags[0:8] == t, heard, 0.0))
-            for s in range(SL):
-                at = slice(s * B, (s + 1) * B)
-                blocks = [sub8[at, (2 * r + h) * B : (2 * r + h + 1) * B] for r in range(RC)]
-                n = h * SL + t
-                value = blocks[0]
-                for r in range(1, RC):
-                    value = jnp.where(which > r - 0.5, blocks[r], value)
-                sub[at, n * B : (n + 1) * B] = value
-
     def panel(h, at):
         return halves(g_ref[h * NCOL : (h + 1) * NCOL, :, at : at + ROWS].reshape(W, ROWS))
 
     gp = [panel(h, 0) for h in range(2)]
     gq = [panel(h, ROWS) for h in range(2)]
+    for s in range(SL):
+        at = slice(s * B, (s + 1) * B)
+        left = [halves(sub[at, h * ROWS : (h + 1) * ROWS]) for h in range(2)]
+        yv[at, :] = dot3(left[0], gp[0], NT) + dot3(left[1], gp[1], NT)
+        zv[at, :] = dot3(left[0], gq[0], NT) + dot3(left[1], gq[1], NT)
+    ring_wait(1, 3)
     topf = c_ref[:, :, 0:W].reshape(W, W)
     top = halves(topf)
     rows = lax.broadcasted_iota(jnp.int32, (B, 1), 0)
     for s in range(SL):
         at = slice(s * B, (s + 1) * B)
-        left = [halves(sub[at, h * ROWS : (h + 1) * ROWS]) for h in range(2)]
-        yp = dot3(left[0], gp[0], NT) + dot3(left[1], gp[1], NT)
-        yy = jnp.where(rows < psz[s], -yp, 0.0)
-        zq = dot3(left[0], gq[0], NT) + dot3(left[1], gq[1], NT)
-        zz = jnp.where(rows < csz[s], -(zq + dot3(halves(yy), top, NN)), 0.0)
+        yy = jnp.where(rows < psz[s], -yv[at, :], 0.0)
+        zz = jnp.where(rows < csz[s], -(zv[at, :] + dot3(halves(yy), top, NN)), 0.0)
         yv[at, :] = yy
         zv[at, :] = zz
         yz[:, :, s * CB : (s + 1) * CB, 0:W] = yy.reshape(NZH, NY, CB, W)
@@ -335,25 +342,90 @@
     sum_step(1)
     e_mat = -dot3(halves(topf.T), halves(u_mat), NN) - dot3(qp, halves(zv[...]), NN)
     put(2, e_mat)
-    sum_step(2)
 
     busy = x < 3
-
-    def xcopy(m, d):
-        return rcopy(acc.at[m], xbuf.at[d - 1], xs.at[d - 1], xr.at[d - 1], xk[d, 0])
+    ahead, behind = xk[1, 0], xk[3, 0]
+    nxt, prv = (x + 1) % NX, (x + 3) % NX
+
+    def xcopy(n, m, part, dev):
+        return rcopy(acc.at[m, part], xbuf.at[n], xs.at[n], xr.at[n], dev)
+
+    def landed(n, dev):
+        rcopy(xbuf.at[n], xbuf.at[n], xs.at[n], xr.at[n], dev).wait_recv()
+
+    def relay_up():
+        return xcopy(0, (x + 2) % NX, 1, ahead)
+
+    def relay_down():
+        return xcopy(1, (x + 2) % NX, 0, behind)
+
+    def plain_up():
+        return xcopy(2, nxt, 0, ahead)
+
+    def plain_down():
+        return xcopy(3, prv, 1, behind)
+
+    def total_up():
+        return xcopy(4, nxt, 1, ahead)
+
+    def total_down():
+        return xcopy(5, prv, 0, behind)
 
     for m in range(3):
         got = kbuf.at[m]
         rcopy(got, got, ks.at[m], kr.at[m], core).wait_recv()
-        acc[m] = aue[k, m] + kbuf[m]
-    for d in (2, 1, 3):
-        m = (x + d) % NX
-
-        @pl.when(m < 3)
+        acc[m] = (aue[k, m] + kbuf[m]).reshape(2, 128, 128)
+        rel = (m + NX - x) % NX
+
+        @pl.when(rel == 2)
         def _():
-            xcopy(m, d).start()
+            relay_up().start()
+            relay_down().start()
+
+        @pl.when(rel == 1)
+        def _():
+            plain_up().start()
+
+        @pl.when(rel == 3)
+        def _():
+            plain_down().start()
+
+    sum_step(2)
+
+    @pl.when(nxt < 3)
+    def _():
+        landed(0, ahead)
+        acc[nxt, 1] = acc[nxt, 1] + xbuf[0]
+        total_up().start()
+
+    @pl.when(prv < 3)
+    def _():
+        landed(1, behind)
+        acc[prv, 0] = acc[prv, 0] + xbuf[1]
+        total_down().start()
 
     sum_step(3)
+
+    def ycopy(d):
+        return rcopy(accx.at[:, (y + d) % NY], ybuf.at[d - 1], ys.at[d - 1], yr.at[d - 1], ydev[d])
+
+    def zcopy(d):
+        return rcopy(accy.at[zpos[d] // NZL], zbuf.at[d - 1], zs.at[d - 1], zr.at[d - 1], zdev[d])
+
+    def fcopy(d, f):
+        n = d * 2 + f - 1
+        return rcopy(auo.at[x, k], auo.at[x, k], fs.at[n], fr.at[n], xk[d, f])
+
+    @pl.when(busy)
+    def _():
+        for n in range(2, 6):
+            landed(n, ahead if n % 2 == 0 else behind)
+        low = acc[x, 0] + (xbuf[2] + xbuf[5])
+        high = acc[x, 1] + (xbuf[3] + xbuf[4])
+        accx[0] = low.reshape(NY, SHARE, 128)
+        accx[1] = high.reshape(NY, SHARE, 128)
+        for d in (4, 3, 5, 2, 6, 1, 7):
+            ycopy(d).start()
 
     for a in range(2):
         n = a * 4 + UPS[a] - 1
@@ -365,29 +437,7 @@
         yzacc[a] = yz[a, y] + (ubuf[n] + dbuf[n2])
     send(yzacc.at[1 - zh], hbuf, hs.at[0], hr.at[0], far)
 
-    def ycopy(d):
-        return rcopy(accx.at[:, (y + d) % NY], ybuf.at[d - 1], ys.at[d - 1], yr.at[d - 1], ydev[d])
-
-    def zcopy(d):
-        return rcopy(accy.at[zpos[d] // NZL], zbuf.at[d - 1], zs.at[d - 1], zr.at[d - 1], zdev[d])
-
-    def fcopy(d, f):
-        n = d * 2 + f - 1
-        return rcopy(auo.at[x, k], auo.at[x, k], fs.at[n], fr.at[n], xk[d, f])
-
-    @pl.when(busy)
-    def _():
-        for d in range(1, NX):
-            xcopy(x, d).wait_recv()
-        total = (acc[x] + xbuf[0]) + (xbuf[1] + xbuf[2])
-        accx[...] = total.reshape(NZH, NY, SHARE, 128)
-        for d in (4, 3, 5, 2, 6, 1, 7):
-            ycopy(d).start()
-
     hop = rcopy(hbuf, hbuf, hs.at[0], hr.at[0], far)
-    hop.wait_recv()
-    yzo[...] = yzacc[zh] + hbuf[...]
-
     @pl.when(busy)
     def _():
         for d in range(1, NY):
@@ -398,6 +448,12 @@
         accy[...] = total
         for d in (4, 3, 5, 2, 6, 1, 7):
             zcopy(d).start()
+
+    hop.wait_recv()
+    yzo[...] = yzacc[zh] + hbuf[...]
+
+    @pl.when(busy)
+    def _():
         for d in range(1, NZ):
             zcopy(d).wait_recv()
         total = accy[zh]
@@ -422,12 +478,21 @@
 
     for copy in sends:
         copy.wait_send()
-    for d in (2, 1, 3):
-        m = (x + d) % NX
-
-        @pl.when(m < 3)
-        def _():
-            xcopy(m, d).wait_send()
+
+    @pl.when((x + 2) % NX < 3)
+    def _():
+        relay_up().wait_send()
+        relay_down().wait_send()
+
+    @pl.when(nxt < 3)
+    def _():
+        plain_up().wait_send()
+        total_up().wait_send()
+
+    @pl.when(prv < 3)
+    def _():
+        plain_down().wait_send()
+        total_down().wait_send()
 
     @pl.when(busy)
     def _():
@@ -457,8 +522,8 @@
         (NZH, NY, rows, 2 * W),
         (2, 3, W, 128),
         (3, W, 128),
-        (3, W, 128),
-        (3, W, 128),
+        (3, 2, 128, 128),
+        (6, 128, 128),
         (NZH, NY, SHARE, 128),
         (NY - 1, NZH, SHARE, 128),
         (NZH, SHARE, 128),
@@ -469,7 +534,7 @@
         (rows, 2 * W),
     ]
     sems = [1, 1, 1, 1, 3, 3, 12, 12, 16, 16, 1, 1, 8, 8, 8, 8]
-    sems += [3, 3, 3, 3, 7, 7, 7, 7, 7, 7, 8, 8, 8, 8, 1, 1]
+    sems += [3, 3, 6, 6, 7, 7, 7, 7, 7, 7, 8, 8, 8, 8, 1, 1]
     return pl.pallas_call(
         step_kernel,
         out_shape=(

time: 78.7 us -> 76.3 us (0.970)
  Pallas kernels: 77.8 us -> 75.4 us
    pallas_call x1, Pallas kernels: 76.3 us -> 73.9 us  [step(): pl.pallas_call(step_kernel, out_shape=(jax.ShapeDtypeStruct((rows, 2 * W)...]
where the time goes in v3:
time: 76.3 us; the launch traced here: 76 us
  Pallas kernels  75.4 us (99%)
    pallas_call x1, Pallas kernels, step(): pl.pallas_call(step_kernel, out_shape=(jax.ShapeDtypeStruct((rows, 2 * W)...  73.9 us

profile of v3, /device:TPU:1, one launch (start us, length us, event | category | flops | bytes accessed | tf_op | source)
XLA Modules:
  0.0 76.0 jit_solution(13450499663363655912)
XLA Ops:
  0.6 73.9 %step.1 = (f32[24,512]{1,0:T(8,128)}, f32[3,2,16,128]{3,2,1,0:T(8,128)}) custom-call(s32[3]{0:T(128)} %pb.3, s32[3]{0:T(128)} %psz.1, s32[3]{0:T(128)} %csz.1, f32[4096,128]{1,0:T(8,128)} %bitcast.9, f32[3,16,128]{2,1,0:T(8,128)} %bitcast.10, f32[3,16,128]{2,1,0:T(8,128)} %bitcast.11, f32[16,256]{1,0:T(8,128)} %top_ref.1, f32[16,256]{1,0:T(8,128)} %d_ref.3), custom_call_target="tpu_custom_call" | custom-call | tf_op jit(solution)/shard_map/step/pallas_call | solution.py:538
  74.6 1.5 %lay.1 = (f32[4,8,256]{2,1,0:T(8,128)}, f32[16,256]{1,0:T(8,128)}, f32[4,8,256]{2,1,0:T(8,128)}, f32[16,256]{1,0:T(8,128)}, f32[16,256]{1,0:T(8,128)}) custom-call(s32[3]{0:T(128)} %pb.3, f32[24,512]{1,0:T(8,128)} %get-tuple-element.12.yz_ref, f32[3,2,16,128]{3,2,1,0:T(8,128)} %get-tuple-element.13.mats_ref, f32[16,256]{1,0:T(8,128)} %d_ref.3, f32[16,256]{1,0:T(8,128)} %cd_ref.1), custom_call_target="tpu_custom_call" | custom-call | tf_op jit(solution)/shard_map/lay/pallas_call | solution.py:575

commit v4 on v3

--- a/solution.py
+++ b/solution.py
@@ -72,11 +72,11 @@
 
 
 def step_kernel(
-    pb, psz, csz, s_hbm, pp_ref, cp_ref, top_ref, d_ref,
+    pb_hbm, psz_hbm, csz_hbm, s_hbm, pp_hbm, cp_hbm, top_hbm, d_hbm,
     yzo, auo,
-    sv, sub8, sub, xv, g_ref, c_ref, yv, zv, uv, yz, aue,
+    pb, psz, csz, pp_ref, cp_ref, d_ref, sv, sub8, sub, xv, g_ref, c_ref, yv, zv, uv, yz, aue,
     kbuf, acc, xbuf, accx, ybuf, accy, zbuf, ubuf, dbuf, yzacc, hbuf,
-    ssem, ps, pr, lsem, gzs, gzr, gxs, gxr, gks, gkr, chs, chr_, cus, cur, cds, cdr,
+    ssem, isem, ps, pr, lsem, gzs, gzr, gxs, gxr, gks, gkr, chs, chr_, cus, cur, cds, cdr,
     ks, kr, xs, xr, ys, yr, zs, zr, fs, fr, us, ur, ds, dr, hs, hr,
 ):
     p, q, x, zl, k, zh, y = place()
@@ -97,20 +97,35 @@
     zdev = [None] + [(row_id(x, zpos[d] % NZL, k), (zpos[d] // NZL) * NY + y) for d in range(1, NZ)]
     far = zdev[NZL]
 
+    barrier = pltpu.get_barrier_semaphore()
+
+    @pl.when(jnp.logical_not(fixed))
+    def _():
+        pl.semaphore_signal(barrier, inc=1, device_id=swap, device_id_type=MESH)
+
+    for dev in zdev[1:] + ydev[1:] + list(xk.values()):
+        pl.semaphore_signal(barrier, inc=1, device_id=dev, device_id_type=MESH)
+
+    loads = [
+        pltpu.make_async_copy(src, dst, isem.at[n])
+        for n, (src, dst) in enumerate((
+            (psz_hbm, psz),
+            (csz_hbm, csz),
+            (pb_hbm, pb),
+            (pp_hbm, pp_ref),
+            (cp_hbm, cp_ref),
+            (top_hbm, xv.at[:, 0:W]),
+            (d_hbm, d_ref),
+        ))
+    ]
+    for load in loads:
+        load.start()
     load_s = pltpu.make_async_copy(s_hbm, sv, ssem.at[0])
     load_s.start()
-
-    barrier = pltpu.get_barrier_semaphore()
-
-    @pl.when(jnp.logical_not(fixed))
-    def _():
-        pl.semaphore_signal(barrier, inc=1, device_id=swap, device_id_type=MESH)
-
-    for dev in zdev[1:] + ydev[1:] + list(xk.values()):
-        pl.semaphore_signal(barrier, inc=1, device_id=dev, device_id_type=MESH)
+    for load in loads:
+        load.wait()
 
     lane = lax.broadcasted_iota(jnp.int32, (SHARE, B), 1)
-    xv[:, 0:W] = top_ref[...]
     for s in range(SL):
         at = W + s * B
         xv[:, at : at + B] = jnp.where(lane < psz[s], pp_ref[s], 0.0)
@@ -200,7 +215,7 @@
 
     def fan(src, dz):
         got = g_ref.at[src]
-        for d in (1, 3) if dz == 0 else (2, 1, 3):
+        for d in (2, 1, 3) if dz == 2 else (1, 3):
             send(got, got, gxs.at[dz * 3 + d - 1], gxr.at[dz * 3 + d - 1], xk[d, 0])
         send(got, got, gks.at[dz * 4], gkr.at[dz * 4], core)
 
@@ -221,7 +236,7 @@
         n = dz * 3 + d - 1
         rcopy(got, got, gxs.at[n], gxr.at[n], xk[d, 0]).wait_recv()
         n = dz * 3 + 1
-        if dz == 0 and d == 1:
+        if (dz, d) in ((0, 1), (1, 3), (3, 3)):
             send(got, got, gxs.at[n], gxr.at[n], xk[d, 0])
         send(got, got, gks.at[dz * 4 + d], gkr.at[dz * 4 + d], core)
 
@@ -240,6 +255,8 @@
     x_wait(3, 1)
     x_wait(3, 3)
 
+    ring_wait(1, 2)
+
     def heard(slot):
         tile = g_ref[slot, 0:8, 2 * ROWS : 2 * ROWS + 128]
         return [jnp.max(jnp.where(tags[0:8] == t, tile, 0.0)) for t in range(SL)]
@@ -262,7 +279,6 @@
     x_wait(2, 1)
     x_wait(2, 3)
     x_wait(2, 2)
-    ring_wait(1, 2)
     for dz in (0, 1, 3, 2):
         for d in (0, 1, 3, 2):
             src = row_id((x + NX - d) % NX, (zl + NZL - dz) % NZL, 1 - k)
@@ -371,24 +387,32 @@
     def total_down():
         return xcopy(5, prv, 0, behind)
 
-    for m in range(3):
+    def merge(m):
         got = kbuf.at[m]
         rcopy(got, got, ks.at[m], kr.at[m], core).wait_recv()
         acc[m] = (aue[k, m] + kbuf[m]).reshape(2, 128, 128)
-        rel = (m + NX - x) % NX
-
-        @pl.when(rel == 2)
-        def _():
-            relay_up().start()
-            relay_down().start()
-
-        @pl.when(rel == 1)
-        def _():
-            plain_up().start()
-
-        @pl.when(rel == 3)
-        def _():
-            plain_down().start()
+
+    opposite = (x + 2) % NX
+
+    @pl.when(opposite < 3)
+    def _():
+        merge(opposite)
+        relay_up().start()
+        relay_down().start()
+
+    @pl.when(nxt < 3)
+    def _():
+        merge(nxt)
+        plain_up().start()
+
+    @pl.when(prv < 3)
+    def _():
+        merge(prv)
+        plain_down().start()
+
+    @pl.when(busy)
+    def _():
+        merge(x)
 
     sum_step(2)
 
@@ -506,10 +530,12 @@
 
 def step(*operands):
     vmem = pl.BlockSpec(memory_space=pltpu.VMEM)
-    smem = pl.BlockSpec(memory_space=pltpu.SMEM)
     dma = pltpu.SemaphoreType.DMA
     rows = SL * CB
     buffers = [
+        (SL, SHARE, B),
+        (SL, SHARE, B),
+        (SHARE, W),
         (RC * B * 8, B),
         (ROWS, 8 * B),
         (ROWS, 2 * ROWS),
@@ -533,7 +559,7 @@
         (NZH, rows, 2 * W),
         (rows, 2 * W),
     ]
-    sems = [1, 1, 1, 1, 3, 3, 12, 12, 16, 16, 1, 1, 8, 8, 8, 8]
+    sems = [1, 7, 1, 1, 1, 3, 3, 12, 12, 16, 16, 1, 1, 8, 8, 8, 8]
     sems += [3, 3, 6, 6, 7, 7, 7, 7, 7, 7, 8, 8, 8, 8, 1, 1]
     return pl.pallas_call(
         step_kernel,
@@ -541,9 +567,11 @@
             jax.ShapeDtypeStruct((rows, 2 * W), F32),
             jax.ShapeDtypeStruct((3, 2, SHARE, 128), F32),
         ),
-        in_specs=[smem] * 3 + [pl.BlockSpec(memory_space=pl.ANY)] + [vmem] * 4,
+        in_specs=[pl.BlockSpec(memory_space=pl.ANY)] * 8,
         out_specs=(vmem, vmem),
-        scratch_shapes=[pltpu.VMEM(b, F32) for b in buffers] + [dma((n,)) for n in sems],
+        scratch_shapes=[pltpu.SMEM((SL,), jnp.int32)] * 3
+        + [pltpu.VMEM(b, F32) for b in buffers]
+        + [dma((n,)) for n in sems],
         compiler_params=pltpu.CompilerParams(collective_id=0, has_side_effects=True),
         name="step",
     )(*operands)

time: 76.3 us -> 74.7 us (0.979)
  Pallas kernels: 75.4 us -> 73.8 us
    pallas_call x1, Pallas kernels: 73.9 us -> 72.4 us  [step(): pl.pallas_call(step_kernel, out_shape=(jax.ShapeDtypeStruct((rows, 2 * W)...]
where the time goes in v4:
time: 74.7 us; the launch traced here: 74.5 us
  Pallas kernels  73.8 us (99%)
    pallas_call x1, Pallas kernels, step(): pl.pallas_call(step_kernel, out_shape=(jax.ShapeDtypeStruct((rows, 2 * W)...  72.4 us

profile of v4, /device:TPU:1, one launch (start us, length us, event | category | flops | bytes accessed | tf_op | source)
XLA Modules:
  0.0 74.5 jit_solution(17002082485129364953)
XLA Ops:
  0.6 72.4 %step.1 = (f32[24,512]{1,0:T(8,128)}, f32[3,2,16,128]{3,2,1,0:T(8,128)}) custom-call(s32[3]{0:T(128)} %pb.1, s32[3]{0:T(128)} %psz_hbm.1, s32[3]{0:T(128)} %csz_hbm.1, f32[4096,128]{1,0:T(8,128)} %bitcast.9, f32[3,16,128]{2,1,0:T(8,128)} %bitcast.10, f32[3,16,128]{2,1,0:T(8,128)} %bitcast.11, f32[16,256]{1,0:T(8,128)} %top_hbm.1, f32[16,256]{1,0:T(8,128)} %d_ref.1), custom_call_target="tpu_custom_call" | custom-call | tf_op jit(solution)/shard_map/step/pallas_call | solution.py:564
  73.0 1.5 %lay.1 = (f32[4,8,256]{2,1,0:T(8,128)}, f32[16,256]{1,0:T(8,128)}, f32[4,8,256]{2,1,0:T(8,128)}, f32[16,256]{1,0:T(8,128)}, f32[16,256]{1,0:T(8,128)}) custom-call(s32[3]{0:T(128)} %pb.1, f32[24,512]{1,0:T(8,128)} %get-tuple-element.12.yz_ref, f32[3,2,16,128]{3,2,1,0:T(8,128)} %get-tuple-element.13.mats_ref, f32[16,256]{1,0:T(8,128)} %d_ref.1, f32[16,256]{1,0:T(8,128)} %cd_ref.1), custom_call_target="tpu_custom_call" | custom-call | tf_op jit(solution)/shard_map/lay/pallas_call | solution.py:603

commit v5 on v4

--- a/solution.py
+++ b/solution.py
@@ -16,9 +16,8 @@
 SHARE = W // NCOL
 ROWS = SL * B
 CB = B // NCOL
-PATCH = 2 * ROWS + 128
-OWN = W + 2 * ROWS
-WIDE = W + PATCH
+PATCH = 2 * ROWS
+OWN = W + PATCH
 UPS = (4, 3)
 DOWNS = (3, 4)
 
@@ -74,7 +73,7 @@
 def step_kernel(
     pb_hbm, psz_hbm, csz_hbm, s_hbm, pp_hbm, cp_hbm, top_hbm, d_hbm,
     yzo, auo,
-    pb, psz, csz, pp_ref, cp_ref, d_ref, sv, sub8, sub, xv, g_ref, c_ref, yv, zv, uv, yz, aue,
+    pb, psz, csz, pp_ref, cp_ref, d_ref, sv, sub8, sub, xv, told, heard, g_ref, c_ref, yv, zv, uv, yz, aue,
     kbuf, acc, xbuf, accx, ybuf, accy, zbuf, ubuf, dbuf, yzacc, hbuf,
     ssem, isem, ps, pr, lsem, gzs, gzr, gxs, gxr, gks, gkr, chs, chr_, cus, cur, cds, cdr,
     ks, kr, xs, xr, ys, yr, zs, zr, fs, fr, us, ur, ds, dr, hs, hr,
@@ -136,8 +135,8 @@
     tags = lax.broadcasted_iota(jnp.int32, (SHARE, 128), 1)
     for s in range(SL):
         tag = jnp.where(tags == s, local[s].astype(F32), tag)
-    xv[:, OWN:WIDE] = tag
-    c_ref[q] = xv[:, 0:OWN]
+    told[...] = tag[0:8]
+    c_ref[q] = xv[...]
 
     pl.semaphore_wait(barrier, 7 + NY - 1 + NZ - 1 + jnp.where(fixed, 0, 1))
 
@@ -148,18 +147,22 @@
         copy.start()
         sends.append(copy)
 
-    piece = xv.at[:, W:WIDE]
-    mine = xv.at[:, 0:OWN]
+    piece = xv.at[:, W:OWN]
+    mine = xv
     out = rcopy(piece, g_ref.at[half * NCOL + q], ps.at[0], pr.at[0], swap)
     keep = pltpu.make_async_copy(piece, g_ref.at[p], lsem.at[0])
+    out_tag = rcopy(told, heard.at[0], ps.at[1], pr.at[1], swap)
+    keep_tag = pltpu.make_async_copy(told, heard.at[0], lsem.at[1])
 
     @pl.when(jnp.logical_not(fixed))
     def _():
         out.start()
+        out_tag.start()
 
     @pl.when(fixed)
     def _():
         keep.start()
+        keep_tag.start()
 
     def ring(a, t, src_up, src_down):
         zz = zh if a == 0 else 1 - zh
@@ -208,10 +211,12 @@
     @pl.when(jnp.logical_not(fixed))
     def _():
         rcopy(piece, g_ref.at[p], ps.at[0], pr.at[0], swap).wait_recv()
+        out_tag.wait_recv()
 
     @pl.when(fixed)
     def _():
         keep.wait()
+        keep_tag.wait()
 
     def fan(src, dz):
         got = g_ref.at[src]
@@ -223,6 +228,7 @@
     for d in (1, 3, 2):
         send(own, own, gzs.at[d - 1], gzr.at[d - 1], lzdev[d])
     fan(p, 0)
+    send(heard.at[0], heard.at[1], gxs.at[12], gxr.at[12], xk[2, 0])
 
     def z_wait(d):
         src = row_id(x, (zl + NZL - d) % NZL, k)
@@ -241,30 +247,31 @@
         send(got, got, gks.at[dz * 4 + d], gkr.at[dz * 4 + d], core)
 
     ring_wait(0, 2)
-    ring_wait(1, 0)
     z_wait(1)
     z_wait(3)
     x_wait(0, 1)
     x_wait(0, 3)
-    ring_wait(1, 1)
+    ring_wait(1, 0)
     z_wait(2)
     x_wait(0, 2)
     ring_wait(0, 3)
     x_wait(1, 1)
     x_wait(1, 3)
+    ring_wait(1, 1)
     x_wait(3, 1)
     x_wait(3, 3)
-
+    x_wait(1, 2)
+    x_wait(3, 2)
+    x_wait(2, 1)
+    x_wait(2, 3)
     ring_wait(1, 2)
-
-    def heard(slot):
-        tile = g_ref[slot, 0:8, 2 * ROWS : 2 * ROWS + 128]
-        return [jnp.max(jnp.where(tags[0:8] == t, tile, 0.0)) for t in range(SL)]
-
-    ours, theirs = heard(p), heard(row_id((x + 2) % NX, zl, k))
+    x_wait(2, 2)
+
+    rcopy(heard.at[1], heard.at[1], gxs.at[12], gxr.at[12], xk[2, 0]).wait_recv()
+    said = [[jnp.max(jnp.where(tags[0:8] == t, heard[h], 0.0)) for t in range(SL)] for h in range(2)]
     for h in range(2):
         for t in range(SL):
-            which = jnp.where(half == h, ours[t], theirs[t])
+            which = jnp.where(half == h, said[0][t], said[1][t])
             for s in range(SL):
                 at = slice(s * B, (s + 1) * B)
                 n = h * SL + t
@@ -274,11 +281,6 @@
                     value = jnp.where(which > r - 0.5, block, value)
                 sub[at, n * B : (n + 1) * B] = value
 
-    x_wait(1, 2)
-    x_wait(3, 2)
-    x_wait(2, 1)
-    x_wait(2, 3)
-    x_wait(2, 2)
     for dz in (0, 1, 3, 2):
         for d in (0, 1, 3, 2):
             src = row_id((x + NX - d) % NX, (zl + NZL - dz) % NZL, 1 - k)
@@ -355,7 +357,6 @@
     uv[mid, :] = uv[mid, :] - first * dot3(halves(d_ref[...]), top, NN)
     u_mat = uv[...]
     put(1, u_mat)
-    sum_step(1)
     e_mat = -dot3(halves(topf.T), halves(u_mat), NN) - dot3(qp, halves(zv[...]), NN)
     put(2, e_mat)
 
@@ -414,6 +415,7 @@
     def _():
         merge(x)
 
+    sum_step(1)
     sum_step(2)
 
     @pl.when(nxt < 3)
@@ -499,6 +501,7 @@
     @pl.when(jnp.logical_not(fixed))
     def _():
         out.wait_send()
+        out_tag.wait_send()
 
     for copy in sends:
         copy.wait_send()
@@ -539,7 +542,9 @@
         (RC * B * 8, B),
         (ROWS, 8 * B),
         (ROWS, 2 * ROWS),
-        (SHARE, WIDE),
+        (SHARE, OWN),
+        (8, 128),
+        (2, 8, 128),
         (NROW, SHARE, PATCH),
         (NCOL, SHARE, OWN),
         (ROWS, W),
@@ -559,7 +564,7 @@
         (NZH, rows, 2 * W),
         (rows, 2 * W),
     ]
-    sems = [1, 7, 1, 1, 1, 3, 3, 12, 12, 16, 16, 1, 1, 8, 8, 8, 8]
+    sems = [1, 7, 2, 2, 2, 3, 3, 13, 13, 16, 16, 1, 1, 8, 8, 8, 8]
     sems += [3, 3, 6, 6, 7, 7, 7, 7, 7, 7, 8, 8, 8, 8, 1, 1]
     return pl.pallas_call(
         step_kernel,

time: 74.7 us -> 73.8 us (0.988)
  Pallas kernels: 73.8 us -> 73 us
    pallas_call x1, Pallas kernels: 72.4 us -> 71.5 us  [step(): pl.pallas_call(step_kernel, out_shape=(jax.ShapeDtypeStruct((rows, 2 * W)...]
where the time goes in v5:
time: 73.8 us; the launch traced here: 73.6 us
  Pallas kernels  73 us (99%)
    pallas_call x1, Pallas kernels, step(): pl.pallas_call(step_kernel, out_shape=(jax.ShapeDtypeStruct((rows, 2 * W)...  71.5 us
    pallas_call x1, Pallas kernels, lay(): pl.pallas_call(place_kernel, out_shape=(rows, share, rows, share, share),...  1.49 us

profile of v5, /device:TPU:1, one launch (start us, length us, event | category | flops | bytes accessed | tf_op | source)
XLA Modules:
  0.0 73.6 jit_solution(13325442576108362520)
XLA Ops:
  0.6 71.5 %step.1 = (f32[24,512]{1,0:T(8,128)}, f32[3,2,16,128]{3,2,1,0:T(8,128)}) custom-call(s32[3]{0:T(128)} %pb.1, s32[3]{0:T(128)} %psz_hbm.1, s32[3]{0:T(128)} %csz_hbm.1, f32[4096,128]{1,0:T(8,128)} %bitcast.9, f32[3,16,128]{2,1,0:T(8,128)} %bitcast.10, f32[3,16,128]{2,1,0:T(8,128)} %bitcast.11, f32[16,256]{1,0:T(8,128)} %top_hbm.1, f32[16,256]{1,0:T(8,128)} %d_ref.1), custom_call_target="tpu_custom_call" | custom-call | tf_op jit(solution)/shard_map/step/pallas_call | solution.py:569
  72.1 1.5 %lay.1 = (f32[4,8,256]{2,1,0:T(8,128)}, f32[16,256]{1,0:T(8,128)}, f32[4,8,256]{2,1,0:T(8,128)}, f32[16,256]{1,0:T(8,128)}, f32[16,256]{1,0:T(8,128)}) custom-call(s32[3]{0:T(128)} %pb.1, f32[24,512]{1,0:T(8,128)} %get-tuple-element.12.yz_ref, f32[3,2,16,128]{3,2,1,0:T(8,128)} %get-tuple-element.13.mats_ref, f32[16,256]{1,0:T(8,128)} %d_ref.1, f32[16,256]{1,0:T(8,128)} %cd_ref.1), custom_call_target="tpu_custom_call" | custom-call | tf_op jit(solution)/shard_map/lay/pallas_call | solution.py:608

commit v6 on v5

--- a/solution.py
+++ b/solution.py
@@ -75,7 +75,7 @@
     yzo, auo,
     pb, psz, csz, pp_ref, cp_ref, d_ref, sv, sub8, sub, xv, told, heard, g_ref, c_ref, yv, zv, uv, yz, aue,
     kbuf, acc, xbuf, accx, ybuf, accy, zbuf, ubuf, dbuf, yzacc, hbuf,
-    ssem, isem, ps, pr, lsem, gzs, gzr, gxs, gxr, gks, gkr, chs, chr_, cus, cur, cds, cdr,
+    ssem, isem, ps, pr, lsem, gzs, gzr, gxs, gxr, gks, gkr, chs, chr_, cus, cur, cds, cdr, cas, car,
     ks, kr, xs, xr, ys, yr, zs, zr, fs, fr, us, ur, ds, dr, hs, hr,
 ):
     p, q, x, zl, k, zh, y = place()
@@ -164,31 +164,27 @@
         keep.start()
         keep_tag.start()
 
-    def ring(a, t, src_up, src_down):
-        zz = zh if a == 0 else 1 - zh
+    def ring(t, src_up, src_down):
         if src_up is not None:
-            at = zz * NY + (y + NY - t) % NY
-            send(src_up, c_ref.at[at], cus.at[a * 4 + t], cur.at[a * 4 + t], up)
+            at = zh * NY + (y + NY - t) % NY
+            send(src_up, c_ref.at[at], cus.at[t], cur.at[t], up)
         if src_down is not None:
-            at = zz * NY + (y + t) % NY
-            send(src_down, c_ref.at[at], cds.at[a * 4 + t], cdr.at[a * 4 + t], down)
-
-    def ring_up_wait(a, t):
-        zz = zh if a == 0 else 1 - zh
-        got = c_ref.at[zz * NY + (y + NY - 1 - t) % NY]
-        rcopy(got, got, cus.at[a * 4 + t], cur.at[a * 4 + t], up).wait_recv()
-        if t + 1 < UPS[a]:
-            ring(a, t + 1, got, None)
-
-    def ring_down_wait(a, t):
-        zz = zh if a == 0 else 1 - zh
-        got = c_ref.at[zz * NY + (y + 1 + t) % NY]
-        rcopy(got, got, cds.at[a * 4 + t], cdr.at[a * 4 + t], down).wait_recv()
-        if t + 1 < DOWNS[a]:
-            ring(a, t + 1, None, got)
+            at = zh * NY + (y + t) % NY
+            send(src_down, c_ref.at[at], cds.at[t], cdr.at[t], down)
+
+    def ring_wait(t):
+        got = c_ref.at[zh * NY + (y + NY - 1 - t) % NY]
+        rcopy(got, got, cus.at[t], cur.at[t], up).wait_recv()
+        if t < 3:
+            ring(t + 1, got, None)
+        if t < 3:
+            got = c_ref.at[zh * NY + (y + 1 + t) % NY]
+            rcopy(got, got, cds.at[t], cdr.at[t], down).wait_recv()
+            if t < 2:
+                ring(t + 1, None, got)
 
     send(mine, c_ref.at[q], chs.at[0], chr_.at[0], far)
-    ring(0, 0, mine, mine)
+    ring(0, mine, mine)
 
     load_s.wait()
     for s in range(SL):
@@ -196,17 +192,12 @@
             blocks = [sv[pl.ds(r * B * 8 + c, B, stride=8), :] for r in range(RC)]
             sub8[s * B : (s + 1) * B, c * B : (c + 1) * B] = pick(blocks, local[s])
 
-    def ring_wait(a, t):
-        if t < UPS[a]:
-            ring_up_wait(a, t)
-        if t < DOWNS[a]:
-            ring_down_wait(a, t)
-
-    ring_wait(0, 0)
-    ring_wait(0, 1)
+    ring_wait(0)
+    ring_wait(1)
     other = c_ref.at[(1 - zh) * NY + y]
     rcopy(other, other, chs.at[0], chr_.at[0], far).wait_recv()
-    ring(1, 0, other, other)
+    for d in (4, 3, 5, 2, 6, 1, 7):
+        send(other, other, cas.at[d - 1], car.at[d - 1], ydev[d])
 
     @pl.when(jnp.logical_not(fixed))
     def _():
@@ -246,25 +237,21 @@
             send(got, got, gxs.at[n], gxr.at[n], xk[d, 0])
         send(got, got, gks.at[dz * 4 + d], gkr.at[dz * 4 + d], core)
 
-    ring_wait(0, 2)
+    ring_wait(2)
     z_wait(1)
     z_wait(3)
     x_wait(0, 1)
     x_wait(0, 3)
-    ring_wait(1, 0)
     z_wait(2)
     x_wait(0, 2)
-    ring_wait(0, 3)
     x_wait(1, 1)
     x_wait(1, 3)
-    ring_wait(1, 1)
     x_wait(3, 1)
     x_wait(3, 3)
     x_wait(1, 2)
     x_wait(3, 2)
     x_wait(2, 1)
     x_wait(2, 3)
-    ring_wait(1, 2)
     x_wait(2, 2)
 
     rcopy(heard.at[1], heard.at[1], gxs.at[12], gxr.at[12], xk[2, 0]).wait_recv()
@@ -297,7 +284,10 @@
         left = [halves(sub[at, h * ROWS : (h + 1) * ROWS]) for h in range(2)]
         yv[at, :] = dot3(left[0], gp[0], NT) + dot3(left[1], gp[1], NT)
         zv[at, :] = dot3(left[0], gq[0], NT) + dot3(left[1], gq[1], NT)
-    ring_wait(1, 3)
+    ring_wait(3)
+    for d in (1, 7, 2, 6, 3, 5, 4):
+        got = c_ref.at[(1 - zh) * NY + (y + NY - d) % NY]
+        rcopy(got, got, cas.at[d - 1], car.at[d - 1], ydev[d]).wait_recv()
     topf = c_ref[:, :, 0:W].reshape(W, W)
     top = halves(topf)
     rows = lax.broadcasted_iota(jnp.int32, (B, 1), 0)
@@ -564,7 +554,7 @@
         (NZH, rows, 2 * W),
         (rows, 2 * W),
     ]
-    sems = [1, 7, 2, 2, 2, 3, 3, 13, 13, 16, 16, 1, 1, 8, 8, 8, 8]
+    sems = [1, 7, 2, 2, 2, 3, 3, 13, 13, 16, 16, 1, 1, 4, 4, 3, 3, 7, 7]
     sems += [3, 3, 6, 6, 7, 7, 7, 7, 7, 7, 8, 8, 8, 8, 1, 1]
     return pl.pallas_call(
         step_kernel,

time: 73.8 us -> 77.6 us (1.051)
  Pallas kernels: 73 us -> 76.8 us
    pallas_call x1, Pallas kernels: 71.5 us -> 75.3 us  [step(): pl.pallas_call(step_kernel, out_shape=(jax.ShapeDtypeStruct((rows, 2 * W)...]
where the time goes in v6:
time: 77.6 us; the launch traced here: 77.4 us
  Pallas kernels  76.8 us (99%)
    pallas_call x1, Pallas kernels, step(): pl.pallas_call(step_kernel, out_shape=(jax.ShapeDtypeStruct((rows, 2 * W)...  75.3 us

profile of v6, /device:TPU:1, one launch (start us, length us, event | category | flops | bytes accessed | tf_op | source)
XLA Modules:
  0.0 77.4 jit_solution(5357709714158445927)
XLA Ops:
  0.6 75.3 %step.1 = (f32[24,512]{1,0:T(8,128)}, f32[3,2,16,128]{3,2,1,0:T(8,128)}) custom-call(s32[3]{0:T(128)} %pb.1, s32[3]{0:T(128)} %psz_hbm.1, s32[3]{0:T(128)} %csz_hbm.1, f32[4096,128]{1,0:T(8,128)} %bitcast.9, f32[3,16,128]{2,1,0:T(8,128)} %bitcast.10, f32[3,16,128]{2,1,0:T(8,128)} %bitcast.11, f32[16,256]{1,0:T(8,128)} %top_hbm.1, f32[16,256]{1,0:T(8,128)} %d_ref.1), custom_call_target="tpu_custom_call" | custom-call | tf_op jit(solution)/shard_map/step/pallas_call | solution.py:559
  75.9 1.5 %lay.1 = (f32[4,8,256]{2,1,0:T(8,128)}, f32[16,256]{1,0:T(8,128)}, f32[4,8,256]{2,1,0:T(8,128)}, f32[16,256]{1,0:T(8,128)}, f32[16,256]{1,0:T(8,128)}) custom-call(s32[3]{0:T(128)} %pb.1, f32[24,512]{1,0:T(8,128)} %get-tuple-element.12.yz_ref, f32[3,2,16,128]{3,2,1,0:T(8,128)} %get-tuple-element.13.mats_ref, f32[16,256]{1,0:T(8,128)} %d_ref.1, f32[16,256]{1,0:T(8,128)} %cd_ref.1), custom_call_target="tpu_custom_call" | custom-call | tf_op jit(solution)/shard_map/lay/pallas_call | solution.py:598

commit v7 on v5

--- a/solution.py
+++ b/solution.py
@@ -18,6 +18,8 @@
 CB = B // NCOL
 PATCH = 2 * ROWS
 OWN = W + PATCH
+RING_UPS = (4, 3, 3)
+RING_DOWNS = (3, 4, 4)
 UPS = (4, 3)
 DOWNS = (3, 4)
 
@@ -164,30 +166,35 @@
         keep.start()
         keep_tag.start()
 
+    def part(a, row):
+        return c_ref.at[row] if a == 0 else c_ref.at[row, :, pl.ds((a - 1) * (OWN // 2), OWN // 2)]
+
+    def ring_row(a, at):
+        return (zh if a == 0 else 1 - zh) * NY + (y + NY + at) % NY
+
     def ring(a, t, src_up, src_down):
-        zz = zh if a == 0 else 1 - zh
+        n = a * 4 + t
         if src_up is not None:
-            at = zz * NY + (y + NY - t) % NY
-            send(src_up, c_ref.at[at], cus.at[a * 4 + t], cur.at[a * 4 + t], up)
+            send(src_up, part(a, ring_row(a, -t)), cus.at[n], cur.at[n], up)
         if src_down is not None:
-            at = zz * NY + (y + t) % NY
-            send(src_down, c_ref.at[at], cds.at[a * 4 + t], cdr.at[a * 4 + t], down)
-
-    def ring_up_wait(a, t):
-        zz = zh if a == 0 else 1 - zh
-        got = c_ref.at[zz * NY + (y + NY - 1 - t) % NY]
-        rcopy(got, got, cus.at[a * 4 + t], cur.at[a * 4 + t], up).wait_recv()
-        if t + 1 < UPS[a]:
-            ring(a, t + 1, got, None)
-
-    def ring_down_wait(a, t):
-        zz = zh if a == 0 else 1 - zh
-        got = c_ref.at[zz * NY + (y + 1 + t) % NY]
-        rcopy(got, got, cds.at[a * 4 + t], cdr.at[a * 4 + t], down).wait_recv()
-        if t + 1 < DOWNS[a]:
-            ring(a, t + 1, None, got)
-
-    send(mine, c_ref.at[q], chs.at[0], chr_.at[0], far)
+            send(src_down, part(a, ring_row(a, t)), cds.at[n], cdr.at[n], down)
+
+    def ring_wait(a, t):
+        n = a * 4 + t
+        if t < RING_UPS[a]:
+            got = part(a, ring_row(a, -1 - t))
+            rcopy(got, got, cus.at[n], cur.at[n], up).wait_recv()
+            if t + 1 < RING_UPS[a]:
+                ring(a, t + 1, got, None)
+        if t < RING_DOWNS[a]:
+            got = part(a, ring_row(a, 1 + t))
+            rcopy(got, got, cds.at[n], cdr.at[n], down).wait_recv()
+            if t + 1 < RING_DOWNS[a]:
+                ring(a, t + 1, None, got)
+
+    for a in (1, 2):
+        side = xv.at[:, pl.ds((a - 1) * (OWN // 2), OWN // 2)]
+        send(side, part(a, q), chs.at[a - 1], chr_.at[a - 1], far)
     ring(0, 0, mine, mine)
 
     load_s.wait()
@@ -196,17 +203,12 @@
             blocks = [sv[pl.ds(r * B * 8 + c, B, stride=8), :] for r in range(RC)]
             sub8[s * B : (s + 1) * B, c * B : (c + 1) * B] = pick(blocks, local[s])
 
-    def ring_wait(a, t):
-        if t < UPS[a]:
-            ring_up_wait(a, t)
-        if t < DOWNS[a]:
-            ring_down_wait(a, t)
-
     ring_wait(0, 0)
     ring_wait(0, 1)
-    other = c_ref.at[(1 - zh) * NY + y]
-    rcopy(other, other, chs.at[0], chr_.at[0], far).wait_recv()
-    ring(1, 0, other, other)
+    for a in (1, 2):
+        other = part(a, (1 - zh) * NY + y)
+        rcopy(other, other, chs.at[a - 1], chr_.at[a - 1], far).wait_recv()
+        ring(a, 0, other, other)
 
     @pl.when(jnp.logical_not(fixed))
     def _():
@@ -252,12 +254,14 @@
     x_wait(0, 1)
     x_wait(0, 3)
     ring_wait(1, 0)
+    ring_wait(2, 0)
     z_wait(2)
     x_wait(0, 2)
     ring_wait(0, 3)
     x_wait(1, 1)
     x_wait(1, 3)
     ring_wait(1, 1)
+    ring_wait(2, 1)
     x_wait(3, 1)
     x_wait(3, 3)
     x_wait(1, 2)
@@ -265,6 +269,7 @@
     x_wait(2, 1)
     x_wait(2, 3)
     ring_wait(1, 2)
+    ring_wait(2, 2)
     x_wait(2, 2)
 
     rcopy(heard.at[1], heard.at[1], gxs.at[12], gxr.at[12], xk[2, 0]).wait_recv()
@@ -298,6 +303,7 @@
         yv[at, :] = dot3(left[0], gp[0], NT) + dot3(left[1], gp[1], NT)
         zv[at, :] = dot3(left[0], gq[0], NT) + dot3(left[1], gq[1], NT)
     ring_wait(1, 3)
+    ring_wait(2, 3)
     topf = c_ref[:, :, 0:W].reshape(W, W)
     top = halves(topf)
     rows = lax.broadcasted_iota(jnp.int32, (B, 1), 0)
@@ -564,7 +570,7 @@
         (NZH, rows, 2 * W),
         (rows, 2 * W),
     ]
-    sems = [1, 7, 2, 2, 2, 3, 3, 13, 13, 16, 16, 1, 1, 8, 8, 8, 8]
+    sems = [1, 7, 2, 2, 2, 3, 3, 13, 13, 16, 16, 2, 2, 12, 12, 12, 12]
     sems += [3, 3, 6, 6, 7, 7, 7, 7, 7, 7, 8, 8, 8, 8, 1, 1]
     return pl.pallas_call(
         step_kernel,

time: 73.8 us -> 74 us (level)
  no operation moved by 1% of the time
where the time goes in v7:
time: 74 us; the launch traced here: 73.8 us
  Pallas kernels  73.1 us (99%)
    pallas_call x1, Pallas kernels, step(): pl.pallas_call(step_kernel, out_shape=(jax.ShapeDtypeStruct((rows, 2 * W)...  71.7 us
    pallas_call x1, Pallas kernels, lay(): pl.pallas_call(place_kernel, out_shape=(rows, share, rows, share, share),...  1.49 us

profile of v7, /device:TPU:1, one launch (start us, length us, event | category | flops | bytes accessed | tf_op | source)
XLA Modules:
  0.0 73.8 jit_solution(2523736379375161923)
XLA Ops:
  0.6 71.7 %step.1 = (f32[24,512]{1,0:T(8,128)}, f32[3,2,16,128]{3,2,1,0:T(8,128)}) custom-call(s32[3]{0:T(128)} %pb.1, s32[3]{0:T(128)} %psz_hbm.1, s32[3]{0:T(128)} %csz_hbm.1, f32[4096,128]{1,0:T(8,128)} %bitcast.9, f32[3,16,128]{2,1,0:T(8,128)} %bitcast.10, f32[3,16,128]{2,1,0:T(8,128)} %bitcast.11, f32[16,256]{1,0:T(8,128)} %top_hbm.1, f32[16,256]{1,0:T(8,128)} %d_ref.1), custom_call_target="tpu_custom_call" | custom-call | tf_op jit(solution)/shard_map/step/pallas_call | solution.py:575
  72.3 1.5 %lay.1 = (f32[4,8,256]{2,1,0:T(8,128)}, f32[16,256]{1,0:T(8,128)}, f32[4,8,256]{2,1,0:T(8,128)}, f32[16,256]{1,0:T(8,128)}, f32[16,256]{1,0:T(8,128)}) custom-call(s32[3]{0:T(128)} %pb.1, f32[24,512]{1,0:T(8,128)} %get-tuple-element.12.yz_ref, f32[3,2,16,128]{3,2,1,0:T(8,128)} %get-tuple-element.13.mats_ref, f32[16,256]{1,0:T(8,128)} %d_ref.1, f32[16,256]{1,0:T(8,128)} %cd_ref.1), custom_call_target="tpu_custom_call" | custom-call | tf_op jit(solution)/shard_map/lay/pallas_call | solution.py:614

commit v8 on v5

--- a/solution.py
+++ b/solution.py
@@ -416,7 +416,6 @@
         merge(x)
 
     sum_step(1)
-    sum_step(2)
 
     @pl.when(nxt < 3)
     def _():
@@ -430,7 +429,7 @@
         acc[prv, 0] = acc[prv, 0] + xbuf[1]
         total_down().start()
 
-    sum_step(3)
+    sum_step(2)
 
     def ycopy(d):
         return rcopy(accx.at[:, (y + d) % NY], ybuf.at[d - 1], ys.at[d - 1], yr.at[d - 1], ydev[d])
@@ -453,6 +452,7 @@
         for d in (4, 3, 5, 2, 6, 1, 7):
             ycopy(d).start()
 
+    sum_step(3)
     for a in range(2):
         n = a * 4 + UPS[a] - 1
         got = ubuf.at[n]

time: 73.8 us -> 72.9 us (0.988)
  Pallas kernels: 73 us -> 72.1 us
    pallas_call x1, Pallas kernels: 71.5 us -> 70.6 us  [step(): pl.pallas_call(step_kernel, out_shape=(jax.ShapeDtypeStruct((rows, 2 * W)...]
where the time goes in v8:
time: 72.9 us; the launch traced here: 72.7 us
  Pallas kernels  72.1 us (99%)
    pallas_call x1, Pallas kernels, step(): pl.pallas_call(step_kernel, out_shape=(jax.ShapeDtypeStruct((rows, 2 * W)...  70.6 us
    pallas_call x1, Pallas kernels, lay(): pl.pallas_call(place_kernel, out_shape=(rows, share, rows, share, share),...  1.49 us

profile of v8, /device:TPU:1, one launch (start us, length us, event | category | flops | bytes accessed | tf_op | source)
XLA Modules:
  0.0 72.7 jit_solution(2423261590025430458)
XLA Ops:
  0.6 70.6 %step.1 = (f32[24,512]{1,0:T(8,128)}, f32[3,2,16,128]{3,2,1,0:T(8,128)}) custom-call(s32[3]{0:T(128)} %pb.1, s32[3]{0:T(128)} %psz_hbm.1, s32[3]{0:T(128)} %csz_hbm.1, f32[4096,128]{1,0:T(8,128)} %bitcast.9, f32[3,16,128]{2,1,0:T(8,128)} %bitcast.10, f32[3,16,128]{2,1,0:T(8,128)} %bitcast.11, f32[16,256]{1,0:T(8,128)} %top_hbm.1, f32[16,256]{1,0:T(8,128)} %d_ref.1), custom_call_target="tpu_custom_call" | custom-call | tf_op jit(solution)/shard_map/step/pallas_call | solution.py:569
  71.2 1.5 %lay.1 = (f32[4,8,256]{2,1,0:T(8,128)}, f32[16,256]{1,0:T(8,128)}, f32[4,8,256]{2,1,0:T(8,128)}, f32[16,256]{1,0:T(8,128)}, f32[16,256]{1,0:T(8,128)}) custom-call(s32[3]{0:T(128)} %pb.1, f32[24,512]{1,0:T(8,128)} %get-tuple-element.12.yz_ref, f32[3,2,16,128]{3,2,1,0:T(8,128)} %get-tuple-element.13.mats_ref, f32[16,256]{1,0:T(8,128)} %d_ref.1, f32[16,256]{1,0:T(8,128)} %cd_ref.1), custom_call_target="tpu_custom_call" | custom-call | tf_op jit(solution)/shard_map/lay/pallas_call | solution.py:608
